TPU v7x, 32 devices: a whole 2x2x4 slice. The times are simulated.
32 devices in a mesh: leaf: 4 (over z), agg: 2 (over core), probe: 4 (over y, x).
Axes of the slice: x: 2, y: 2, z: 4, core: 2. Of those that a mesh axis runs over, the one named last changes fastest.
Arguments:
- probes: float32 [4, 192, 1024], P('probe', None, ('leaf', 'agg')), may hold values from -16 to 16
- viscosity: float32 [192, 1024], P(None, ('leaf', 'agg')), may hold values from 0.1 to 10
- friction: float32 [192, 1024], P(None, ('leaf', 'agg')), may hold values from 0.05 to 1
- sensitivity: float32 [192, 1024], P(None, ('leaf', 'agg')), may hold values from 0.5 to 3
- misfit_weight: float32 [192, 1024], P(None, ('leaf', 'agg')), may hold values from 1 to 10
- grad_ref: float32 [192, 192], replicated, may hold values from -2 to 3, as said below
- trace_ref: float32 [192, 192], replicated, may hold values from -2 to 3
- coarse_modes: float32 [192, 128], replicated, may hold values from -0.4375 to 0.4375
- coarse_inv: float32 [64, 128, 128], P(('leaf', 'agg')), may hold values from -1 to 5, as said below
- peer_slots: int32 [8, 8, 16], P(('leaf', 'agg')), may hold values from -1 to 127, as said below
- local_pairs: int32 [2, 1024], P(None, ('leaf', 'agg')), may hold values from 0 to 127, as said below
- elem_agg: int32 [1024], P(('leaf', 'agg')), may hold values from 0 to 15
Outputs:
- incr_velocity: float32 [4, 192, 1024], P('probe', None, ('leaf', 'agg'))
- hess_action: float32 [4, 192, 1024], P('probe', None, ('leaf', 'agg'))
- trace_est: float32 [], replicated
Inputs may be any that keep to these rules, and one draw needn't show every extreme that they name: `grad_ref`: nonsingular. `coarse_inv`: each block is symmetric positive definite. peer_slots[P, Q, s] >= 0 exactly when peer_slots[Q, P, s] >= 0; the filled slots of a pair come first; no slot of a pair P, P is filled; the partitions are blocks of a three-dimensional grid and only blocks that touch by a face, edge or corner share slots, so a partition has at most 26 partners; some pair of partitions fills all 16 slots. `local_pairs`: the two elements of a pair differ.
All inputs are finite; a program needn't handle non-finite values.
Results may differ from a plain program's by a relative error of at most 0.0003.
Values sent between devices are 32-bit elements; how exact they have to be, the bound alone decides.
No kernel may reach another device: no remote copies, remote signals or barrier semaphores. Data moves between devices by JAX's collectives and lax.ppermute only.
A program may use at most 64 MiB of HBM per device.

v0:
```python
import jax
import jax.numpy as jnp
from jax import lax
from jax.experimental import pallas as pl
from jax.experimental.pallas import tpu as pltpu
from jax.sharding import PartitionSpec as P


ITERS = 2
SWEEPS = 3


highest = lax.Precision.HIGHEST
relax_weight = 0.6
f32 = jnp.float32
bf16 = jnp.bfloat16


def matmul(left, right):
    return jnp.dot(left, right, precision=highest, preferred_element_type=jnp.float32)


def distributed(
    probes,
    viscosity,
    friction,
    sensitivity,
    misfit_weight,
    grad_ref,
    trace_ref,
    coarse_modes,
    coarse_inv,
    peer_slots,
    local_pairs,
    elem_agg,
):
    agg_count = lax.axis_size("agg")
    elem_local = viscosity.shape[1]
    slot_flat = peer_slots.reshape(-1)
    filled = slot_flat >= 0
    own_local = jnp.where(filled, slot_flat, 0)
    filled_float = filled.astype(jnp.float32)
    first_end = local_pairs[0]
    second_end = local_pairs[1]
    counts = jnp.zeros((elem_local,), jnp.float32)
    counts = counts.at[first_end].add(1.0).at[second_end].add(1.0).at[own_local].add(filled_float)
    trace_square = jnp.sum(trace_ref * trace_ref, axis=0)
    diag_op = (
        matmul((grad_ref * grad_ref).T, viscosity)
        + friction
        + counts[None, :] * trace_square[:, None]
    )
    group_aggs = agg_count * coarse_inv.shape[0]
    one_hot = (elem_agg[:, None] == jnp.arange(group_aggs, dtype=jnp.int32)[None, :]).astype(
        jnp.float32
    )

    def operate(field_vec):
        inner_term = matmul(grad_ref.T, viscosity * matmul(grad_ref, field_vec))
        traces = matmul(trace_ref, field_vec)
        outgoing = traces[:, own_local] * filled_float[None, :]
        incoming = lax.all_to_all(
            outgoing, ("leaf", "agg"), split_axis=1, concat_axis=1, tiled=True
        )
        cross_diff = outgoing - incoming
        local_diff = traces[:, first_end] - traces[:, second_end]
        accumulated = jnp.zeros_like(field_vec)
        accumulated = (
            accumulated.at[:, first_end].add(local_diff).at[:, second_end].add(-local_diff)
        )
        accumulated = accumulated.at[:, own_local].add(cross_diff)
        return inner_term + friction * field_vec + matmul(trace_ref.T, accumulated)

    def coarse(residual_now):
        projected = matmul(coarse_modes.T, residual_now)
        coarse_sums = matmul(projected, one_hot)
        own_sums = lax.psum_scatter(coarse_sums, "agg", scatter_dimension=1, tiled=True)
        solved_own = jnp.einsum("acd,da->ca", coarse_inv, own_sums, precision=highest)
        solved_all = lax.all_gather(solved_own, "agg", axis=1, tiled=True)
        return matmul(coarse_modes, matmul(solved_all, one_hot.T))

    def precond(residual_now):
        smooth = relax_weight * residual_now / diag_op
        for _ in range(SWEEPS - 1):
            smooth = smooth + relax_weight * (residual_now - operate(smooth)) / diag_op
        return smooth + coarse(residual_now)

    def energy_sum(left, right):
        return lax.psum(jnp.sum(left * right), ("leaf", "agg"))

    def krylov(source):
        residual_now = source
        precon = precond(residual_now)
        search = precon
        energy_now = energy_sum(residual_now, precon)
        iterate = jnp.zeros_like(source)
        for iteration in range(ITERS):
            image_vec = operate(search)
            step_size = energy_now / lax.psum(jnp.sum(search * image_vec), ("leaf", "agg"))
            iterate = iterate + step_size * search
            if iteration + 1 < ITERS:
                residual_now = residual_now - step_size * image_vec
                precon = precond(residual_now)
                energy_next = energy_sum(residual_now, precon)
                search = precon + energy_next / energy_now * search
                energy_now = energy_next
        return iterate

    probe_field = probes[0]
    forward = krylov(sensitivity * probe_field)
    adjoint = krylov(misfit_weight * forward)
    action = sensitivity * adjoint
    trace_value = lax.psum(jnp.sum(probe_field * action), ("leaf", "agg", "probe")) / lax.axis_size(
        "probe"
    )
    return (forward[None], action[None], trace_value)


def split(value):
    high = value.astype(bf16)
    low = (value - high.astype(f32)).astype(bf16)
    return high, low


def dot(left, right):
    return jnp.dot(left, right, preferred_element_type=f32)


def dot_nt(left, right):
    return lax.dot_general(left, right, (((1,), (1,)), ((), ())), preferred_element_type=f32)


def total(value):
    return jnp.sum(jnp.sum(value, axis=0, keepdims=True), axis=1, keepdims=True)


def spec(space):
    return pl.BlockSpec(memory_space=space)


VM = pltpu.VMEM
SM = pltpu.SMEM


def call(kernel, outs, args, spaces=None, scratch=(), flops=0, bytes_accessed=0):
    return kernel_call(kernel, outs, args, spaces, scratch, flops, bytes_accessed)


def kernel_call(kernel, outs, args, spaces, scratch, flops, bytes_accessed):
    spaces = spaces or [VM] * len(args)
    args = [
        pltpu.with_memory_space_constraint(arg, space) if space == pltpu.HBM else arg
        for arg, space in zip(args, spaces)
    ]
    return pl.pallas_call(
        kernel,
        out_shape=[jax.ShapeDtypeStruct(*one) for one in outs],
        in_specs=[spec(space) for space in spaces],
        out_specs=[spec(VM) for _ in outs],
        scratch_shapes=list(scratch),
        compiler_params=pltpu.CompilerParams(vmem_limit_bytes=16 * 1024 * 1024),
        cost_estimate=pl.CostEstimate(
            flops=flops, bytes_accessed=bytes_accessed, transcendentals=0
        ),
    )(*args)


class Dims:
    def __init__(self, ndof, elem, parts, cap, modes, aggs):
        self.ndof, self.elem, self.parts, self.cap = ndof, elem, parts, cap
        self.modes, self.aggs = modes, aggs
        self.total = elem * parts
        self.half = parts // 2
        self.group = 2 * aggs
        self.all_aggs = parts * aggs
        self.chunk = 2 * elem


def prepare_constants(dim, grad, trace, modes, g3, gs, gsq3, my, m3t, trsq):
    n = dim.ndof
    high, low = split(grad)
    g3[:, 0:n], g3[:, n : 2 * n], g3[:, 2 * n :] = high, high, low
    gt = grad.T
    tt = trace.T
    gram = lax.dot_general(
        tt, tt, (((1,), (1,)), ((), ())), precision=highest, preferred_element_type=f32
    )
    gh, gl = split(gt)
    sh, sl = split(gram)
    for place, piece in enumerate((gh, sh, gh, sh, gl, sl)):
        gs[:, place * n : (place + 1) * n] = piece
    qh, ql = split(gt * gt)
    gsq3[:, 0:n], gsq3[:, n : 2 * n], gsq3[:, 2 * n :] = qh, qh, ql
    mh, ml = split(modes)
    w = dim.modes
    my[:, 0:w], my[:, w : 2 * w], my[:, 2 * w :] = mh, mh, ml
    th, tl = split(modes.T)
    m3t[:, 0:n], m3t[:, n : 2 * n], m3t[:, 2 * n :] = th, th, tl
    trsq[...] = jnp.sum(tt * tt, axis=1, keepdims=True)


def restrict(field, hot, m3t):
    high, low = split(field)
    sums = dot_nt(high, hot) + dot_nt(low, hot)
    high, low = split(sums)
    return dot(m3t[...], jnp.concatenate([high, low, high], axis=0))


def solve_blocks(sums, first, inv, count):
    rows = []
    for index in range(count):
        column = sums[:, first + index : first + index + 1]
        rows.append(jnp.sum(inv[index] * column, axis=0, keepdims=True))
    return jnp.concatenate(rows, axis=0)


def hot_of(dim, agg_row, agg_index, columns):
    place = lax.broadcasted_iota(jnp.int32, (dim.group, columns), 0)
    wanted = lax.rem(place + agg_index * dim.aggs, dim.group)
    return jnp.where(wanted.astype(f32) == agg_row, 1.0, 0.0).astype(bf16)


def source_kernel(
    dim, probe_in, sens_in, pairs_in, slots_in, agg_in, grad_in, trace_in, modes_in, inv_in,
    visc_in, payload, sums, g3, gs, gsq3, my, m3t, trsq, inv,
    probe, sens, pairs, slots, agg_row, grad, trace, modes, sems,
):
    moves = (
        (probe_in.at[0], probe),
        (sens_in, sens),
        (pairs_in, pairs),
        (slots_in.at[0], slots),
        (agg_in, agg_row),
        (grad_in, grad),
        (trace_in, trace),
        (modes_in, modes),
        (inv_in, inv),
        (visc_in, payload.at[pl.ds(dim.ndof + 8, dim.ndof)]),
    )
    copies = [
        pltpu.make_async_copy(src, dst, sems.at[index]) for index, (src, dst) in enumerate(moves)
    ]
    for copy in copies:
        copy.start()
    for copy in copies:
        copy.wait()
    n = dim.ndof
    value = probe[...] * sens[...]
    payload[0:n, :] = value
    agg_float = agg_row[...].astype(f32)
    payload[n : n + 2, :] = pairs[...].astype(f32)
    for part in range(dim.parts):
        span = slice(part * dim.cap, (part + 1) * dim.cap)
        payload[n + 2 : n + 3, span] = slots[part : part + 1, :].astype(f32)
    payload[n + 3 : n + 4, :] = agg_float
    payload[n + 4 : n + 8, :] = jnp.zeros((4, dim.elem), f32)
    prepare_constants(dim, grad[...], trace[...], modes[...], g3, gs, gsq3, my, m3t, trsq)
    hot = hot_of(dim, agg_float, 0, dim.elem)
    sums[...] = restrict(value, hot, m3t)


def source_coarse_kernel(
    dim, place, sums_own, sums_partner, inv_own, inv_partner, fric_in, out, sem
):
    n = dim.ndof
    copy = pltpu.make_async_copy(fric_in, out.at[pl.ds(0, n)], sem)
    copy.start()
    agg = place[1]
    sums = sums_own[...] + sums_partner[...]
    first, second = sums[:, 0 : dim.aggs], sums[:, dim.aggs :]
    mine = jnp.where(agg == 0, first, second)
    theirs = jnp.where(agg == 0, second, first)
    out[pl.ds(pl.multiple_of(n + agg * dim.aggs, dim.aggs), dim.aggs), :] = solve_blocks(
        mine, 0, inv_own, dim.aggs
    )
    out[pl.ds(pl.multiple_of(n + (1 - agg) * dim.aggs, dim.aggs), dim.aggs), :] = solve_blocks(
        theirs, 0, inv_partner, dim.aggs
    )
    copy.wait()


def build_kernel(dim, place, *refs):
    blocks = refs[: dim.parts]
    source, visc, lap, hot2, counts, hot_own, table, sides, agg = refs[dim.parts :]
    n, e = dim.ndof, dim.elem
    for index, ref in enumerate(blocks):
        where = place[4 + index]
        columns = pl.ds(pl.multiple_of(where * e, e), e)
        source[:, columns] = ref[0:n, :]
        visc[:, columns] = ref[n + 8 : 2 * n + 8, :]
        sides[pl.ds(where, 1), :] = ref[n : n + 1, :]
        sides[pl.ds(where + dim.parts, 1), :] = ref[n + 1 : n + 2, :]
        table[pl.ds(where, 1), :] = ref[n + 2 : n + 3, :]
        group = (where // 2) * dim.group
        agg[:, columns] = ref[n + 3 : n + 4, :] + group.astype(f32)
    elem_id = lax.broadcasted_iota(jnp.int32, (e, e), 0).astype(f32)
    lane = lax.broadcasted_iota(jnp.int32, (e, e), 1)
    column_id = lax.broadcasted_iota(jnp.int32, (e, e), 1)
    row_id = lax.broadcasted_iota(jnp.int32, (e, e), 0)
    on_diagonal = row_id == column_id
    full = table[...]
    rolled = [full]
    for shift in range(1, dim.parts):
        rolled.append(pltpu.roll(full, shift * dim.cap, 1))
    slot_block = lane // dim.cap
    for p in range(dim.parts):
        mine = jnp.where(full[p : p + 1, :] == elem_id, 1.0, 0.0).astype(bf16)
        first = jnp.where(sides[p : p + 1, :] == elem_id, 1.0, 0.0)
        second = jnp.where(sides[p + dim.parts : p + dim.parts + 1, :] == elem_id, 1.0, 0.0)
        edge = (first - second).astype(bf16)
        local = dot_nt(edge, edge)
        count = jnp.sum(mine.astype(f32), axis=1, keepdims=True)
        for q in range(dim.parts):
            if q == p:
                block = local + jnp.where(on_diagonal, count, 0.0)
                diagonal = jnp.where(on_diagonal, block, 0.0)
                counts[:, p * e : (p + 1) * e] = jnp.sum(diagonal, axis=0, keepdims=True)
            else:
                row = rolled[(q - p) % dim.parts][q : q + 1, :]
                theirs = jnp.where((row == elem_id) & (slot_block == q), 1.0, 0.0).astype(bf16)
                block = -dot_nt(mine, theirs)
            lap[p * e : (p + 1) * e, q * e : (q + 1) * e] = block.astype(bf16)
    agg_id = lax.broadcasted_iota(jnp.int32, (dim.all_aggs, dim.total), 0).astype(f32)
    hot2[...] = jnp.where(agg[...] == agg_id, 1.0, 0.0).astype(bf16)
    leaf = place[0]
    span = 2 * e
    own_row = agg[:, pl.ds(pl.multiple_of(leaf * span, span), span)]
    own_row = own_row - (leaf * dim.group).astype(f32)
    hot_own[...] = hot_of(dim, own_row, place[1], span)


def chunks(dim):
    return [slice(start, start + dim.chunk) for start in range(0, dim.total, dim.chunk)]


def apply_operator(dim, vec, consts, v3, uy, emit):
    visc, fric, lap, g3, gs = consts
    n = dim.ndof
    for c in chunks(dim):
        high, low = split(vec[:, c])
        v3[0:n, c] = high
        v3[n : 2 * n, c] = low
        v3[2 * n : 3 * n, c] = high
    for c in chunks(dim):
        high, low = split(visc[:, c] * dot(g3[...], v3[:, c]))
        uy[0:n, c] = high
        uy[2 * n : 3 * n, c] = low
        uy[4 * n : 5 * n, c] = high
    for c in chunks(dim):
        both = dot(v3[0 : 2 * n, :], lap[:, c])
        high, low = split(both[0:n] + both[n : 2 * n])
        uy[n : 2 * n, c] = high
        uy[3 * n : 4 * n, c] = low
        uy[5 * n : 6 * n, c] = high
    for c in chunks(dim):
        emit(c, dot(gs[...], uy[:, c]) + fric[:, c] * vec[:, c])


def smooth_loop(dim, resid, smooth, w_diag, consts, v3, uy):
    for c in chunks(dim):
        smooth[:, c] = w_diag[:, c] * resid[:, c]

    def sweep(index, carry):
        def emit(c, image):
            smooth[:, c] = smooth[:, c] + w_diag[:, c] * (resid[:, c] - image)

        apply_operator(dim, smooth, consts, v3, uy, emit)
        return carry

    lax.fori_loop(0, SWEEPS - 1, sweep, 0)


def coarse_add(dim, solved, my, hot2, target):
    high, low = split(solved)
    coarse = dot_nt(my[...], jnp.concatenate([high, low, high], axis=1))
    high, low = split(coarse)
    for c in chunks(dim):
        target[:, c] = target[:, c] + dot(high, hot2[:, c]) + dot(low, hot2[:, c])


def group_solve(dim, place, resid, hot_own, m3t, inv_own, inv_partner, out):
    leaf, agg = place[0], place[1]
    span = 2 * dim.elem
    field = resid[:, pl.ds(pl.multiple_of(leaf * span, span), span)]
    sums = restrict(field, hot_own[...], m3t)
    out[pl.ds(pl.multiple_of(agg * dim.aggs, dim.aggs), dim.aggs), :] = solve_blocks(
        sums, 0, inv_own, dim.aggs
    )
    out[pl.ds(pl.multiple_of((1 - agg) * dim.aggs, dim.aggs), dim.aggs), :] = solve_blocks(
        sums, dim.aggs, inv_partner, dim.aggs
    )


def first_step(dim, source, image, consts, v3, uy, resid, search, scal):
    def emit(c, value):
        image[:, c] = value

    apply_operator(dim, search, consts, v3, uy, emit)
    energy = total(source[...] * search[...])
    step = energy / total(search[...] * image[...])
    resid[...] = source[...] - step * image[...]
    scal[0:1, :] = jnp.broadcast_to(energy, (1, 128))
    scal[1:2, :] = jnp.broadcast_to(step, (1, 128))


def second_step(dim, resid, search, precon, scal, consts, v3, uy, image):
    energy = total(resid[...] * precon[...])
    ratio = energy / scal[0:1, 0:1]
    precon[...] = precon[...] + ratio * search[...]

    def emit(c, value):
        image[:, c] = value

    apply_operator(dim, precon, consts, v3, uy, emit)
    step = energy / total(precon[...] * image[...])
    precon[...] = scal[1:2, 0:1] * search[...] + step * precon[...]


def gather_parts(dim, place, parts, solved):
    groups = []
    for ref in parts:
        skip = ref.shape[0] % dim.ndof
        first = ref.shape[0] - skip
        groups += [(ref, first + step) for step in range(0, skip, dim.group)]
    for index, (ref, first) in enumerate(groups):
        where = place[4 + index] // 2
        solved[pl.ds(pl.multiple_of(where * dim.group, dim.group), dim.group), :] = ref[
            first : first + dim.group, :
        ]


def begin_kernel(dim, place, source, visc, counts, trsq, lap, g3, gs, gsq3, *refs):
    n, e = dim.ndof, dim.elem
    fric_blocks = refs[: dim.parts]
    fric, w_diag, smooth, v3, uy = refs[dim.parts :]
    for index in range(dim.parts):
        columns = pl.ds(pl.multiple_of(place[4 + index] * e, e), e)
        fric[:, columns] = fric_blocks[index][0:n, :]
    for c in chunks(dim):
        high, low = split(visc[:, c])
        diag = dot(gsq3[...], jnp.concatenate([high, low, high], axis=0))
        diag = diag + fric[:, c] + counts[:, c] * trsq[...]
        w_diag[:, c] = relax_weight / diag
    smooth_loop(dim, source, smooth, w_diag, (visc, fric, lap, g3, gs), v3, uy)


def sweep_kernel(dim, first, resid, visc, fric, w_diag, lap, g3, gs, *refs):
    if first:
        smooth, v3, uy, start = refs
        for c in chunks(dim):
            start[:, c] = w_diag[:, c] * resid[:, c]
    else:
        start, smooth, v3, uy = refs

    def emit(c, image):
        smooth[:, c] = start[:, c] + w_diag[:, c] * (resid[:, c] - image)

    apply_operator(dim, start, (visc, fric, lap, g3, gs), v3, uy, emit)


def middle_kernel(
    dim, place, smooth, resid, search, scal, visc, fric, lap, g3, gs, hot2, my, m3t,
    hot_own, inv_own, inv_partner, *refs,
):
    weights = refs[: dim.parts]
    parts = refs[dim.parts : -8]
    iterate, source, out, v3, uy, image, solved, precon = refs[-8:]
    e = dim.elem
    gather_parts(dim, place, parts, solved)
    precon[...] = smooth[...]
    coarse_add(dim, solved[...], my, hot2, precon)
    consts = (visc, fric, lap, g3, gs)
    second_step(dim, resid, search, precon, scal, consts, v3, uy, image)
    mine = pl.ds(pl.multiple_of(place[4] * e, e), e)
    iterate[...] = precon[:, mine]
    for index, ref in enumerate(weights):
        columns = pl.ds(pl.multiple_of(place[4 + index] * e, e), e)
        source[:, columns] = ref[...] * precon[:, columns]
    group_solve(dim, place, source, hot_own, m3t, inv_own, inv_partner, out)


def step_kernel(
    dim, place, smooth, source, visc, fric, lap, g3, gs, hot2, my, m3t, hot_own, inv_own,
    inv_partner, *refs,
):
    parts = refs[:-8]
    search, resid, scal, out, v3, uy, image, solved = refs[-8:]
    gather_parts(dim, place, parts, solved)
    search[...] = smooth[...]
    coarse_add(dim, solved[...], my, hot2, search)
    consts = (visc, fric, lap, g3, gs)
    first_step(dim, source, image, consts, v3, uy, resid, search, scal)
    group_solve(dim, place, resid, hot_own, m3t, inv_own, inv_partner, out)


def final_kernel(
    dim, place, smooth, resid, search, scal, source, sens, visc, fric, lap, g3, gs, hot2, my, *refs
):
    parts = refs[:-7]
    action, trace, v3, uy, image, solved, precon = refs[-7:]
    e = dim.elem
    gather_parts(dim, place, parts, solved)
    precon[...] = smooth[...]
    coarse_add(dim, solved[...], my, hot2, precon)
    consts = (visc, fric, lap, g3, gs)
    second_step(dim, resid, search, precon, scal, consts, v3, uy, image)
    mine = pl.ds(pl.multiple_of(place[4] * e, e), e)
    action[...] = sens[...] * precon[:, mine]
    trace[...] = jnp.broadcast_to(total(source[...] * precon[...]), (1, 128))


def replicated(
    probes,
    viscosity,
    friction,
    sensitivity,
    misfit_weight,
    grad_ref,
    trace_ref,
    coarse_modes,
    coarse_inv,
    peer_slots,
    local_pairs,
    elem_agg,
):
    leaf_count = lax.axis_size("leaf")
    dim = Dims(
        viscosity.shape[0],
        viscosity.shape[1],
        2 * leaf_count,
        peer_slots.shape[2],
        coarse_modes.shape[1],
        coarse_inv.shape[0],
    )
    n, e, ne = dim.ndof, dim.elem, dim.total
    leaf, agg = lax.axis_index("leaf"), lax.axis_index("agg")
    order = jnp.arange(dim.half, dtype=jnp.int32)
    chips = leaf ^ order
    place = jnp.concatenate(
        [
            jnp.stack([leaf, agg, leaf, agg]),
            chips * 2 + agg,
            chips * 2 + (1 - agg),
        ]
    ).astype(jnp.int32)
    flip = [(0, 1), (1, 0)]

    def to_partner(value):
        return lax.ppermute(value, "agg", flip)

    def peers(value):
        found = [value]
        for step in range(1, leaf_count):
            pairs = [(index, index ^ step) for index in range(leaf_count)]
            found.append(lax.ppermute(value, "leaf", pairs))
        return found

    def gather(value):
        own = peers(value)
        return own + [to_partner(one) for one in own]

    payload, sums, g3, gs, gsq3, my, m3t, trsq, inv_own = call(
        lambda *refs: source_kernel(dim, *refs),
        [
            ((2 * n + 8, e), f32),
            ((dim.modes, dim.group), f32),
            ((n, 3 * n), bf16),
            ((n, 6 * n), bf16),
            ((n, 3 * n), bf16),
            ((n, 3 * dim.modes), bf16),
            ((dim.modes, 3 * n), bf16),
            ((n, 1), f32),
            (coarse_inv.shape, f32),
        ],
        [probes, sensitivity, local_pairs, peer_slots, elem_agg.reshape(1, e)]
        + [grad_ref, trace_ref, coarse_modes, coarse_inv, viscosity],
        [pltpu.HBM] * 10,
        scratch=[
            VM((n, e), f32),
            VM((n, e), f32),
            VM((2, e), jnp.int32),
            VM((dim.parts, dim.cap), jnp.int32),
            VM((1, e), jnp.int32),
            VM((n, n), f32),
            VM((n, n), f32),
            VM((n, dim.modes), f32),
            pltpu.SemaphoreType.DMA((10,)),
        ],
        flops=10**8,
    )
    source_blocks = gather(payload)
    inv_partner = to_partner(inv_own)
    sums_partner = to_partner(sums)
    (second_payload,) = call(
        lambda *refs: source_coarse_kernel(dim, *refs),
        [((n + dim.group, e), f32)],
        [place, sums, sums_partner, inv_own, inv_partner, friction],
        [SM, VM, VM, VM, VM, pltpu.HBM],
        scratch=[pltpu.SemaphoreType.DMA(())],
    )
    parts = peers(second_payload)
    fric_blocks = parts + [to_partner(one) for one in parts]
    own = peers(misfit_weight)
    weight_blocks = own + [to_partner(one) for one in own]

    field = ((n, ne), f32)
    source, visc, lap, hot2, counts, hot_own = call(
        lambda *refs: build_kernel(dim, *refs),
        [
            field,
            field,
            ((ne, ne), bf16),
            ((dim.all_aggs, ne), bf16),
            ((1, ne), f32),
            ((dim.group, 2 * e), bf16),
        ],
        [place] + source_blocks,
        [SM] + [VM] * dim.parts,
        scratch=[VM((dim.parts, e), f32), VM((2 * dim.parts, e), f32), VM((1, ne), f32)],
    )
    work = [VM((3 * n, ne), bf16), VM((6 * n, ne), bf16)]
    image = VM((n, ne), f32)
    solved = VM((dim.all_aggs, dim.modes), f32)
    scal_shape = ((8, 128), f32)
    out_shape = ((dim.group, dim.modes), f32)
    once = 2 * ne * n * (9 * n + 2 * ne)

    fric, w_diag, smooth = call(
        lambda *refs: begin_kernel(dim, *refs),
        [field] * 3,
        [place, source, visc, counts, trsq, lap, g3, gs, gsq3] + fric_blocks,
        [SM] + [VM] * (8 + dim.parts),
        scratch=work,
        flops=2 * once,
    )

    def sweep_of(first, args):
        (found,) = call(
            lambda *refs: sweep_kernel(dim, first, *refs),
            [field],
            args,
            scratch=work + ([image] if first else []),
            flops=once,
        )
        return found

    def smooth_and_spread(value, solved_group):
        consts = [value, visc, fric, w_diag, lap, g3, gs]
        smooth, found = None, solved_group
        parts = [solved_group]
        for sweep in range(SWEEPS - 1):
            width = 2**sweep
            if width < leaf_count:
                pairs = [(index, index ^ width) for index in range(leaf_count)]
                other = lax.ppermute(found, "leaf", pairs)
                parts.append(other)
                if 2 * width < leaf_count:
                    found = jnp.concatenate([found, other], axis=0)
            smooth = sweep_of(sweep == 0, consts if sweep == 0 else consts + [smooth])
        return smooth, parts

    def step_of(smooth, start, parts):
        return call(
            lambda *refs: step_kernel(dim, *refs),
            [field, field, scal_shape, out_shape],
            [place, smooth, start, visc, fric, lap, g3, gs, hot2, my, m3t, hot_own, inv_own]
            + [inv_partner]
            + parts,
            [SM] + [VM] * (13 + len(parts)),
            scratch=work + [image, solved],
            flops=once,
        )

    search, resid, scal, out = step_of(smooth, source, parts)
    smooth, parts = smooth_and_spread(resid, out)
    iterate, source_two, out = call(
        lambda *refs: middle_kernel(dim, *refs),
        [((n, e), f32), field, out_shape],
        [place, smooth, resid, search, scal, visc, fric, lap, g3, gs, hot2, my]
        + [m3t, hot_own, inv_own, inv_partner]
        + weight_blocks
        + parts,
        [SM] + [VM] * (15 + dim.parts + len(parts)),
        scratch=work + [image, solved, image],
        flops=once,
    )
    smooth, parts = smooth_and_spread(source_two, out)
    search, resid, scal, out = step_of(smooth, source_two, parts)
    smooth, parts = smooth_and_spread(resid, out)
    action, trace = call(
        lambda *refs: final_kernel(dim, *refs),
        [((n, e), f32), ((1, 128), f32)],
        [place, smooth, resid, search, scal, source, sensitivity, visc, fric, lap, g3, gs, hot2]
        + [my]
        + parts,
        [SM] + [VM] * (13 + len(parts)),
        scratch=work + [image, solved, image],
        flops=once,
    )
    probe_count = lax.axis_size("probe")
    traces = [trace]
    for step in range(1, probe_count):
        pairs = [(index, (index + step) % probe_count) for index in range(probe_count)]
        if probe_count & (probe_count - 1) == 0:
            pairs = [(index, index ^ step) for index in range(probe_count)]
        traces.append(lax.ppermute(trace, "probe", pairs))
    trace_value = sum(one[0, 0] for one in traces) / probe_count
    return iterate[None], action[None], trace_value


def fits_one_core(mesh, viscosity, coarse_modes, coarse_inv, peer_slots, local_pairs):
    leaf_count, agg_count = mesh.shape["leaf"], mesh.shape["agg"]
    ndof, elem = viscosity.shape
    parts = leaf_count * agg_count
    cap = peer_slots.shape[2]
    aggs = coarse_inv.shape[0]
    return (
        agg_count == 2
        and leaf_count & (leaf_count - 1) == 0
        and leaf_count <= 2 ** (SWEEPS - 1)
        and elem == 128
        and coarse_modes.shape[1] == 128
        and parts * cap == elem
        and local_pairs.shape[1] == elem
        and ndof % 16 == 0
        and aggs % 8 == 0
        and local_pairs.shape[1] + (parts - 1) * cap <= 256
        and parts * elem <= 1024
    )


def solution(mesh):
    in_specs = (
        P("probe", None, ("leaf", "agg")),
        P(None, ("leaf", "agg")),
        P(None, ("leaf", "agg")),
        P(None, ("leaf", "agg")),
        P(None, ("leaf", "agg")),
        P(),
        P(),
        P(),
        P(("leaf", "agg"), None, None),
        P(("leaf", "agg"), None, None),
        P(None, ("leaf", "agg")),
        P(("leaf", "agg")),
    )
    out_specs = (P("probe", None, ("leaf", "agg")), P("probe", None, ("leaf", "agg")), P())

    def on_device(*args):
        if fits_one_core(mesh, args[1], args[7], args[8], args[9], args[10]):
            return replicated(*args)
        return distributed(*args)

    return jax.shard_map(
        on_device, mesh=mesh, in_specs=in_specs, out_specs=out_specs, check_vma=False
    )
```

profile of v0, /device:TPU:0, one launch (start us, length us, event | category | flops | bytes accessed | tf_op | source)
XLA Modules:
  0.0 112.8 jit_solution(5786628184961211856)
XLA Ops:
  0.6 2.2 %shard_map.139 = (f32[392,128]{1,0:T(8,128)S(1)}, f32[128,16]{1,0:T(8,128)S(1)}, bf16[192,576]{1,0:T(8,128)(2,1)S(1)}, bf16[192,1152]{1,0:T(8,128)(2,1)S(1)}, bf...) custom-call(f32[1,192,128]{2,1,0:T(8,128)} %refs_0_.1, ...), custom_call_target="tpu_custom_call" | custom-call | flops 100000000 | tf_op jit(solution)/shard_map/pallas_call | solution.py:155
  4.7 4.6 %collective-permute-start.2 = (f32[392,128]{1,0:T(8,128)S(1)}, f32[392,128]{1,0:T(8,128)S(1)}, u32[]{:S(2)}, u32[]{:S(2)}) collective-permute-start(f32[392,128]{1,0:T(8,128)S(1)} %get-tuple-element.34.refs_1_), channel_id=1, source_target_pairs={{0,24},{8,16},{16,8},{24,0},{1,25},{9,17},{17,9},{25,1},{2,26},{10... | collective-permute-start | bytes 602120 | tf_op jit(solution)/shard_map/ppermute | solution.py:555
  11.7 3.8 %collective-permute-start.18 = (f32[192,128]{1,0:T(8,128)}, f32[192,128]{1,0:T(8,128)}, u32[]{:S(2)}, u32[]{:S(2)}) collective-permute-start(f32[192,128]{1,0:T(8,128)} %refs_16_.1), channel_id=1, source_target_pairs={{0,24},{8,16},{16,8},{24,0},{1,25},{9,17},{17,9},{25,1},{2,26},{10... | collective-permute-start | bytes 294920 | tf_op jit(solution)/shard_map/ppermute | solution.py:555
  15.5 10.4 %collective-permute-done.18.refs_19_ = f32[192,128]{1,0:T(8,128)} collective-permute-done((f32[192,128]{1,0:T(8,128)}, f32[192,128]{1,0:T(8,128)}, u32[]{:S(2)}, u32[]{:S(2)}) %collective-permute-start.18) | collective-permute-done | bytes 98336 | tf_op jit(solution)/shard_map/ppermute | solution.py:555
  26.4 3.1 %collective-permute-done.1.refs_3_ = f32[392,128]{1,0:T(8,128)S(1)} collective-permute-done((f32[392,128]{1,0:T(8,128)S(1)}, f32[392,128]{1,0:T(8,128)S(1)}, u32[]{:S(2)}, u32[]{:S(2)}) %collective-permute-start.1) | collective-permute-done | bytes 200736 | tf_op jit(solution)/shard_map/ppermute | solution.py:555
  29.5 3.8 %collective-permute-start.17 = (f32[192,128]{1,0:T(8,128)}, f32[192,128]{1,0:T(8,128)}, u32[]{:S(2)}, u32[]{:S(2)}) collective-permute-start(f32[192,128]{1,0:T(8,128)} %refs_16_.1), channel_id=1, source_target_pairs={{0,16},{8,24},{16,0},{24,8},{1,17},{9,25},{17,1},{25,9},{2,18},{10... | collective-permute-start | bytes 294920 | tf_op jit(solution)/shard_map/ppermute | solution.py:555
  39.9 3.3 %collective-permute-start.9 = (f32[208,128]{1,0:T(8,128)S(1)}, f32[208,128]{1,0:T(8,128)S(1)}, u32[]{:S(2)}, u32[]{:S(2)}) collective-permute-start(f32[208,128]{1,0:T(8,128)S(1)} %shard_map.141.refs_9_.refs_14_), channel_id=1, source_target_pairs={{0,8},{8,0},{16,24},{24,16},{1,9},{9,1},{17,25},{25,17},{2,10},{10... | collective-permute-start | bytes 319496 | tf_op jit(solution)/shard_map/ppermute | solution.py:555
  43.2 3.3 %collective-permute-done.11.refs_12_.refs_17_ = f32[208,128]{1,0:T(8,128)S(1)} collective-permute-done((f32[208,128]{1,0:T(8,128)S(1)}, f32[208,128]{1,0:T(8,128)S(1)}, u32[]{:S(2)}, u32[]{:S(2)}) %collective-permute-start.11) | collective-permute-done | bytes 106528 | tf_op jit(solution)/shard_map/ppermute | solution.py:555
  46.5 3.2 %collective-permute-done.10.refs_11_.refs_16_ = f32[208,128]{1,0:T(8,128)S(1)} collective-permute-done((f32[208,128]{1,0:T(8,128)S(1)}, f32[208,128]{1,0:T(8,128)S(1)}, u32[]{:S(2)}, u32[]{:S(2)}) %collective-permute-start.10) | collective-permute-done | bytes 106528 | tf_op jit(solution)/shard_map/ppermute | solution.py:555
  50.2 2.6 %shard_map.140 = (f32[192,1024]{1,0:T(8,128)S(1)}, f32[192,1024]{1,0:T(8,128)S(1)}, bf16[1024,1024]{1,0:T(8,128)(2,1)S(1)}, bf16[64,1024]{1,0:T(8,128)(2,1)S(1)}...) custom-call(s32[12]{0:T(128)S(1)} %concatenate.12.refs_0_, f32[392,128]{1,0:T(8,128)S(1)} %get-tuple-element.34.refs_1_, ...), custom_call_target="tpu_custom_call" | custom-call | tf_op jit(solution)/shard_map/pallas_call | solution.py:155
  52.8 2.2 %collective-permute-done.16.refs_17_ = f32[192,128]{1,0:T(8,128)S(1)} collective-permute-done((f32[192,128]{1,0:T(8,128)S(1)}, f32[192,128]{1,0:T(8,128)S(1)}, u32[]{:S(2)}, u32[]{:S(2)}) %collective-permute-start.16) | collective-permute-done | bytes 98336 | tf_op jit(solution)/shard_map/ppermute | solution.py:555
  56.0 5.4 %shard_map.142 = (f32[192,1024]{1,0:T(8,128)S(1)}, f32[192,1024]{1,0:T(8,128)S(1)}, f32[192,1024]{1,0:T(8,128)S(1)}) custom-call(s32[12]{0:T(128)S(1)} %concatenate.12.refs_0_, f32[192,1024]{1,0:T(8,128)S(1)} %get-tuple-element.35.refs_1_.refs_2_.refs_5_, f32[192,1024]{1,0:T(8,128)S(1)} %get-tuple-element.36.refs_2_.refs_3_.refs_1_.refs_5_.refs_7_, ...), custom_call_target="tpu_custom_call" | custom-call | flops 2969567232 | tf_op jit(solution)/shard_map/pallas_call | solution.py:155
  61.4 4.0 %shard_map.143 = (f32[192,1024]{1,0:T(8,128)S(1)}, f32[192,1024]{1,0:T(8,128)S(1)}, f32[8,128]{1,0:T(8,128)S(1)}, f32[16,128]{1,0:T(8,128)S(1)}) custom-call(s32[12]{0:T(128)S(1)} %concatenate.12.refs_0_, f32[192,1024]{1,0:T(8,128)S(1)} %get-tuple-element.45.refs_1_, f32[192,1024]{1,0:T(8,128)S(1)} %get-tuple-element.35.refs_1_.refs_2_.refs_5_, ...), custom_call_target="tpu_custom_call" | custom-call | flops 1484783616 | tf_op jit(solution)/shard_map/pallas_call | solution.py:155
  65.8 2.0 %shard_map.144.refs_7_ = f32[192,1024]{1,0:T(8,128)S(1)} custom-call(f32[192,1024]{1,0:T(8,128)S(1)} %get-tuple-element.51.refs_0_.refs_2_, f32[192,1024]{1,0:T(8,128)S(1)} %get-tuple-element.36.refs_2_.refs_3_.refs_1_.refs_5_.refs_7_, f32[192,1024]{1,0:T(8,128)S(1)} %get-tuple-element.46.refs_4_.refs_2_.refs_6_.refs_8_, ...), custom_call_target="tpu_custom_call" | custom-call | flops 1484783616 | tf_op jit(solution)/shard_map/pallas_call | solution.py:155
  70.4 2.0 %shard_map.145.refs_1_ = f32[192,1024]{1,0:T(8,128)S(1)} custom-call(f32[192,1024]{1,0:T(8,128)S(1)} %get-tuple-element.51.refs_0_.refs_2_, f32[192,1024]{1,0:T(8,128)S(1)} %get-tuple-element.36.refs_2_.refs_3_.refs_1_.refs_5_.refs_7_, f32[192,1024]{1,0:T(8,128)S(1)} %get-tuple-element.46.refs_4_.refs_2_.refs_6_.refs_8_, ...), custom_call_target="tpu_custom_call" | custom-call | flops 1484783616 | tf_op jit(solution)/shard_map/pallas_call | solution.py:155
  73.9 4.8 %shard_map.146 = (f32[192,128]{1,0:T(8,128)}, f32[192,1024]{1,0:T(8,128)S(1)}, f32[16,128]{1,0:T(8,128)S(1)}) custom-call(s32[12]{0:T(128)S(1)} %concatenate.12.refs_0_, f32[192,1024]{1,0:T(8,128)S(1)} %shard_map.145.refs_1_, f32[192,1024]{1,0:T(8,128)S(1)} %get-tuple-element.51.refs_0_.refs_2_, f32[192,1024]{1,0:T(8,128)S(1)} %get-tuple-element.53.refs_3_, ...), custom_call_target="tpu_custom_call" | custom-call | flops 1484783616 | tf_op jit(solution)/shard_map/pallas_call | solution.py:155
  79.2 2.0 %shard_map.147.refs_7_ = f32[192,1024]{1,0:T(8,128)S(1)} custom-call(f32[192,1024]{1,0:T(8,128)S(1)} %get-tuple-element.57.refs_0_.refs_2_, f32[192,1024]{1,0:T(8,128)S(1)} %get-tuple-element.36.refs_2_.refs_3_.refs_1_.refs_5_.refs_7_, f32[192,1024]{1,0:T(8,128)S(1)} %get-tuple-element.46.refs_4_.refs_2_.refs_6_.refs_8_, ...), custom_call_target="tpu_custom_call" | custom-call | flops 1484783616 | tf_op jit(solution)/shard_map/pallas_call | solution.py:155
  83.7 2.0 %shard_map.148.refs_1_ = f32[192,1024]{1,0:T(8,128)S(1)} custom-call(f32[192,1024]{1,0:T(8,128)S(1)} %get-tuple-element.57.refs_0_.refs_2_, f32[192,1024]{1,0:T(8,128)S(1)} %get-tuple-element.36.refs_2_.refs_3_.refs_1_.refs_5_.refs_7_, f32[192,1024]{1,0:T(8,128)S(1)} %get-tuple-element.46.refs_4_.refs_2_.refs_6_.refs_8_, ...), custom_call_target="tpu_custom_call" | custom-call | flops 1484783616 | tf_op jit(solution)/shard_map/pallas_call | solution.py:155
  85.7 1.6 %collective-permute-done.26.refs_16_ = f32[32,128]{1,0:T(8,128)S(1)} collective-permute-done((f32[32,128]{1,0:T(8,128)S(1)}, f32[32,128]{1,0:T(8,128)S(1)}, u32[]{:S(2)}, u32[]{:S(2)}) %collective-permute-start.26) | collective-permute-done | bytes 16416 | tf_op jit(solution)/shard_map/ppermute | solution.py:655
  87.2 4.2 %shard_map.149 = (f32[192,1024]{1,0:T(8,128)S(1)}, f32[192,1024]{1,0:T(8,128)S(1)}, f32[8,128]{1,0:T(8,128)S(1)}, f32[16,128]{1,0:T(8,128)S(1)}) custom-call(s32[12]{0:T(128)S(1)} %concatenate.12.refs_0_, f32[192,1024]{1,0:T(8,128)S(1)} %shard_map.148.refs_1_, f32[192,1024]{1,0:T(8,128)S(1)} %get-tuple-element.57.refs_0_.refs_2_, ...), custom_call_target="tpu_custom_call" | custom-call | flops 1484783616 | tf_op jit(solution)/shard_map/pallas_call | solution.py:155
  91.9 2.0 %shard_map.150.refs_7_ = f32[192,1024]{1,0:T(8,128)S(1)} custom-call(f32[192,1024]{1,0:T(8,128)S(1)} %get-tuple-element.59.refs_0_.refs_2_, f32[192,1024]{1,0:T(8,128)S(1)} %get-tuple-element.36.refs_2_.refs_3_.refs_1_.refs_5_.refs_7_, f32[192,1024]{1,0:T(8,128)S(1)} %get-tuple-element.46.refs_4_.refs_2_.refs_6_.refs_8_, ...), custom_call_target="tpu_custom_call" | custom-call | flops 1484783616 | tf_op jit(solution)/shard_map/pallas_call | solution.py:155
  96.4 2.0 %shard_map.151.refs_1_ = f32[192,1024]{1,0:T(8,128)S(1)} custom-call(f32[192,1024]{1,0:T(8,128)S(1)} %get-tuple-element.59.refs_0_.refs_2_, f32[192,1024]{1,0:T(8,128)S(1)} %get-tuple-element.36.refs_2_.refs_3_.refs_1_.refs_5_.refs_7_, f32[192,1024]{1,0:T(8,128)S(1)} %get-tuple-element.46.refs_4_.refs_2_.refs_6_.refs_8_, ...), custom_call_target="tpu_custom_call" | custom-call | flops 1484783616 | tf_op jit(solution)/shard_map/pallas_call | solution.py:155
  100.0 4.2 %shard_map.152 = (f32[192,128]{1,0:T(8,128)}, f32[1,128]{1,0:T(1,128)S(1)}) custom-call(s32[12]{0:T(128)S(1)} %concatenate.12.refs_0_, f32[192,1024]{1,0:T(8,128)S(1)} %shard_map.151.refs_1_, f32[192,1024]{1,0:T(8,128)S(1)} %get-tuple-element.59.refs_0_.refs_2_, f32[192,1024]{1,0:T(8,128)S(1)} %get-tuple-element.60.refs_3_, ...), custom_call_target="tpu_custom_call" | custom-call | flops 1484783616 | tf_op jit(solution)/shard_map/pallas_call | solution.py:155
  109.3 2.4 %collective-permute-done.31 = f32[1,128]{1,0:T(1,128)S(1)} collective-permute-done((f32[1,128]{1,0:T(1,128)S(1)}, f32[1,128]{1,0:T(1,128)S(1)}, u32[]{:S(2)}, u32[]{:S(2)}) %collective-permute-start.31) | collective-permute-done | bytes 544 | tf_op jit(solution)/shard_map/ppermute | solution.py:706
  (79 shorter events, 29.6 us)
Async XLA Ops:
  4.2 29.2 %collective-permute-start.8 = (f32[8,128,128]{2,1,0:T(8,128)S(1)}, f32[8,128,128]{2,1,0:T(8,128)S(1)}, u32[]{:S(2)}, u32[]{:S(2)}) collective-permute-start(f32[8,128,128]{2,1,0:T(8,128)S(1)} %get-tuple-element.44.refs_3_.refs_12_.refs_14_), channel_id=1, source_target_pairs={{0,4},{4,0},{1,5},{5,1},{2,6},{6,2},{3,7},{7,3},{8,12},{12,8},{9,1... | collective-permute-start | bytes 1572872 | tf_op jit(solution)/shard_map/ppermute | solution.py:549
  4.7 21.3 %collective-permute-start.2 = (f32[392,128]{1,0:T(8,128)S(1)}, f32[392,128]{1,0:T(8,128)S(1)}, u32[]{:S(2)}, u32[]{:S(2)}) collective-permute-start(f32[392,128]{1,0:T(8,128)S(1)} %get-tuple-element.34.refs_1_), channel_id=1, source_target_pairs={{0,24},{8,16},{16,8},{24,0},{1,25},{9,17},{17,9},{25,1},{2,26},{10... | collective-permute-start | bytes 602120 | tf_op jit(solution)/shard_map/ppermute | solution.py:555
  9.2 20.3 %collective-permute-start.1 = (f32[392,128]{1,0:T(8,128)S(1)}, f32[392,128]{1,0:T(8,128)S(1)}, u32[]{:S(2)}, u32[]{:S(2)}) collective-permute-start(f32[392,128]{1,0:T(8,128)S(1)} %get-tuple-element.34.refs_1_), channel_id=1, source_target_pairs={{0,16},{8,24},{16,0},{24,8},{1,17},{9,25},{17,1},{25,9},{2,18},{10... | collective-permute-start | bytes 602120 | tf_op jit(solution)/shard_map/ppermute | solution.py:555
  9.2 24.1 %collective-permute-start = (f32[392,128]{1,0:T(8,128)S(1)}, f32[392,128]{1,0:T(8,128)S(1)}, u32[]{:S(2)}, u32[]{:S(2)}) collective-permute-start(f32[392,128]{1,0:T(8,128)S(1)} %get-tuple-element.34.refs_1_), channel_id=1, source_target_pairs={{0,8},{8,0},{16,24},{24,16},{1,9},{9,1},{17,25},{25,17},{2,10},{10... | collective-permute-start | bytes 602120 | tf_op jit(solution)/shard_map/ppermute | solution.py:555
  11.7 14.2 %collective-permute-start.18 = (f32[192,128]{1,0:T(8,128)}, f32[192,128]{1,0:T(8,128)}, u32[]{:S(2)}, u32[]{:S(2)}) collective-permute-start(f32[192,128]{1,0:T(8,128)} %refs_16_.1), channel_id=1, source_target_pairs={{0,24},{8,16},{16,8},{24,0},{1,25},{9,17},{17,9},{25,1},{2,26},{10... | collective-permute-start | bytes 294920 | tf_op jit(solution)/shard_map/ppermute | solution.py:555
  25.9 13.8 %collective-permute-start.3 = (f32[392,128]{1,0:T(8,128)S(1)}, f32[392,128]{1,0:T(8,128)S(1)}, u32[]{:S(2)}, u32[]{:S(2)}) collective-permute-start(f32[392,128]{1,0:T(8,128)S(1)} %get-tuple-element.34.refs_1_), channel_id=1, source_target_pairs={{0,4},{4,0},{1,5},{5,1},{2,6},{6,2},{3,7},{7,3},{8,12},{12,8},{9,1... | collective-permute-start | bytes 602120 | tf_op jit(solution)/shard_map/ppermute | solution.py:549
  25.9 14.0 %collective-permute-start.6 = (f32[392,128]{1,0:T(8,128)S(1)}, f32[392,128]{1,0:T(8,128)S(1)}, u32[]{:S(2)}, u32[]{:S(2)}) collective-permute-start(f32[392,128]{1,0:T(8,128)S(1)} %collective-permute-done.2.refs_4_), channel_id=1, source_target_pairs={{0,4},{4,0},{1,5},{5,1},{2,6},{6,2},{3,7},{7,3},{8,12},{12,8},{9,1... | collective-permute-start | bytes 602120 | tf_op jit(solution)/shard_map/ppermute | solution.py:549
  29.5 9.3 %collective-permute-start.17 = (f32[192,128]{1,0:T(8,128)}, f32[192,128]{1,0:T(8,128)}, u32[]{:S(2)}, u32[]{:S(2)}) collective-permute-start(f32[192,128]{1,0:T(8,128)} %refs_16_.1), channel_id=1, source_target_pairs={{0,16},{8,24},{16,0},{24,8},{1,17},{9,25},{17,1},{25,9},{2,18},{10... | collective-permute-start | bytes 294920 | tf_op jit(solution)/shard_map/ppermute | solution.py:555
  33.4 9.8 %collective-permute-start.5 = (f32[392,128]{1,0:T(8,128)S(1)}, f32[392,128]{1,0:T(8,128)S(1)}, u32[]{:S(2)}, u32[]{:S(2)}) collective-permute-start(f32[392,128]{1,0:T(8,128)S(1)} %collective-permute-done.1.refs_3_), channel_id=1, source_target_pairs={{0,4},{4,0},{1,5},{5,1},{2,6},{6,2},{3,7},{7,3},{8,12},{12,8},{9,1... | collective-permute-start | bytes 602120 | tf_op jit(solution)/shard_map/ppermute | solution.py:549
  33.4 16.8 %collective-permute-start.4 = (f32[392,128]{1,0:T(8,128)S(1)}, f32[392,128]{1,0:T(8,128)}, u32[]{:S(2)}, u32[]{:S(2)}) collective-permute-start(f32[392,128]{1,0:T(8,128)S(1)} %collective-permute-done.refs_2_), channel_id=1, source_target_pairs={{0,4},{4,0},{1,5},{5,1},{2,6},{6,2},{3,7},{7,3},{8,12},{12,8},{9,1... | collective-permute-start | bytes 602120 | tf_op jit(solution)/shard_map/ppermute | solution.py:549
  38.8 7.7 %collective-permute-start.11 = (f32[208,128]{1,0:T(8,128)S(1)}, f32[208,128]{1,0:T(8,128)S(1)}, u32[]{:S(2)}, u32[]{:S(2)}) collective-permute-start(f32[208,128]{1,0:T(8,128)S(1)} %shard_map.141.refs_9_.refs_14_), channel_id=1, source_target_pairs={{0,24},{8,16},{16,8},{24,0},{1,25},{9,17},{17,9},{25,1},{2,26},{10... | collective-permute-start | bytes 319496 | tf_op jit(solution)/shard_map/ppermute | solution.py:555
  39.7 10.0 %collective-permute-start.10 = (f32[208,128]{1,0:T(8,128)S(1)}, f32[208,128]{1,0:T(8,128)S(1)}, u32[]{:S(2)}, u32[]{:S(2)}) collective-permute-start(f32[208,128]{1,0:T(8,128)S(1)} %shard_map.141.refs_9_.refs_14_), channel_id=1, source_target_pairs={{0,16},{8,24},{16,0},{24,8},{1,17},{9,25},{17,1},{25,9},{2,18},{10... | collective-permute-start | bytes 319496 | tf_op jit(solution)/shard_map/ppermute | solution.py:555
  39.9 9.8 %collective-permute-start.9 = (f32[208,128]{1,0:T(8,128)S(1)}, f32[208,128]{1,0:T(8,128)S(1)}, u32[]{:S(2)}, u32[]{:S(2)}) collective-permute-start(f32[208,128]{1,0:T(8,128)S(1)} %shard_map.141.refs_9_.refs_14_), channel_id=1, source_target_pairs={{0,8},{8,0},{16,24},{24,16},{1,9},{9,1},{17,25},{25,17},{2,10},{10... | collective-permute-start | bytes 319496 | tf_op jit(solution)/shard_map/ppermute | solution.py:555
  43.2 11.7 %collective-permute-start.12 = (f32[208,128]{1,0:T(8,128)S(1)}, f32[208,128]{1,0:T(8,128)S(1)}, u32[]{:S(2)}, u32[]{:S(2)}) collective-permute-start(f32[208,128]{1,0:T(8,128)S(1)} %shard_map.141.refs_9_.refs_14_), channel_id=1, source_target_pairs={{0,4},{4,0},{1,5},{5,1},{2,6},{6,2},{3,7},{7,3},{8,12},{12,8},{9,1... | collective-permute-start | bytes 319496 | tf_op jit(solution)/shard_map/ppermute | solution.py:549
  46.5 9.0 %collective-permute-start.15 = (f32[208,128]{1,0:T(8,128)S(1)}, f32[208,128]{1,0:T(8,128)S(1)}, u32[]{:S(2)}, u32[]{:S(2)}) collective-permute-start(f32[208,128]{1,0:T(8,128)S(1)} %collective-permute-done.11.refs_12_.refs_17_), channel_id=1, source_target_pairs={{0,4},{4,0},{1,5},{5,1},{2,6},{6,2},{3,7},{7,3},{8,12},{12,8},{9,1... | collective-permute-start | bytes 319496 | tf_op jit(solution)/shard_map/ppermute | solution.py:549
  49.7 5.9 %collective-permute-start.14 = (f32[208,128]{1,0:T(8,128)S(1)}, f32[208,128]{1,0:T(8,128)S(1)}, u32[]{:S(2)}, u32[]{:S(2)}) collective-permute-start(f32[208,128]{1,0:T(8,128)S(1)} %collective-permute-done.10.refs_11_.refs_16_), channel_id=1, source_target_pairs={{0,4},{4,0},{1,5},{5,1},{2,6},{6,2},{3,7},{7,3},{8,12},{12,8},{9,1... | collective-permute-start | bytes 319496 | tf_op jit(solution)/shard_map/ppermute | solution.py:549
  49.7 6.3 %collective-permute-start.13 = (f32[208,128]{1,0:T(8,128)S(1)}, f32[208,128]{1,0:T(8,128)S(1)}, u32[]{:S(2)}, u32[]{:S(2)}) collective-permute-start(f32[208,128]{1,0:T(8,128)S(1)} %collective-permute-done.9.refs_10_.refs_15_), channel_id=1, source_target_pairs={{0,4},{4,0},{1,5},{5,1},{2,6},{6,2},{3,7},{7,3},{8,12},{12,8},{9,1... | collective-permute-start | bytes 319496 | tf_op jit(solution)/shard_map/ppermute | solution.py:549
  50.2 4.8 %collective-permute-start.16 = (f32[192,128]{1,0:T(8,128)S(1)}, f32[192,128]{1,0:T(8,128)S(1)}, u32[]{:S(2)}, u32[]{:S(2)}) collective-permute-start(f32[192,128]{1,0:T(8,128)S(1)} %copy-done.1), channel_id=1, source_target_pairs={{0,8},{8,0},{16,24},{24,16},{1,9},{9,1},{17,25},{25,17},{2,10},{10... | collective-permute-start | bytes 294920 | tf_op jit(solution)/shard_map/ppermute | solution.py:555
  55.0 17.4 %collective-permute-start.19 = (f32[192,128]{1,0:T(8,128)S(1)}, f32[192,128]{1,0:T(8,128)S(1)}, u32[]{:S(2)}, u32[]{:S(2)}) collective-permute-start(f32[192,128]{1,0:T(8,128)S(1)} %copy-done.1), channel_id=1, source_target_pairs={{0,4},{4,0},{1,5},{5,1},{2,6},{6,2},{3,7},{7,3},{8,12},{12,8},{9,1... | collective-permute-start | bytes 294920 | tf_op jit(solution)/shard_map/ppermute | solution.py:549
  55.0 17.4 %collective-permute-start.22 = (f32[192,128]{1,0:T(8,128)}, f32[192,128]{1,0:T(8,128)S(1)}, u32[]{:S(2)}, u32[]{:S(2)}) collective-permute-start(f32[192,128]{1,0:T(8,128)} %collective-permute-done.18.refs_19_), channel_id=1, source_target_pairs={{0,4},{4,0},{1,5},{5,1},{2,6},{6,2},{3,7},{7,3},{8,12},{12,8},{9,1... | collective-permute-start | bytes 294920 | tf_op jit(solution)/shard_map/ppermute | solution.py:549
  55.5 16.9 %collective-permute-start.21 = (f32[192,128]{1,0:T(8,128)}, f32[192,128]{1,0:T(8,128)S(1)}, u32[]{:S(2)}, u32[]{:S(2)}) collective-permute-start(f32[192,128]{1,0:T(8,128)} %collective-permute-done.17.refs_18_), channel_id=1, source_target_pairs={{0,4},{4,0},{1,5},{5,1},{2,6},{6,2},{3,7},{7,3},{8,12},{12,8},{9,1... | collective-permute-start | bytes 294920 | tf_op jit(solution)/shard_map/ppermute | solution.py:549
  55.6 16.8 %collective-permute-start.20 = (f32[192,128]{1,0:T(8,128)S(1)}, f32[192,128]{1,0:T(8,128)S(1)}, u32[]{:S(2)}, u32[]{:S(2)}) collective-permute-start(f32[192,128]{1,0:T(8,128)S(1)} %collective-permute-done.16.refs_17_), channel_id=1, source_target_pairs={{0,4},{4,0},{1,5},{5,1},{2,6},{6,2},{3,7},{7,3},{8,12},{12,8},{9,1... | collective-permute-start | bytes 294920 | tf_op jit(solution)/shard_map/ppermute | solution.py:549
  69.2 4.7 %collective-permute-start.24 = (f32[32,128]{1,0:T(8,128)S(1)}, f32[32,128]{1,0:T(8,128)S(1)}, u32[]{:S(2)}, u32[]{:S(2)}) collective-permute-start(f32[32,128]{1,0:T(8,128)S(1)} %pad_maximum_fusion), channel_id=1, source_target_pairs={{0,16},{8,24},{16,0},{24,8},{1,17},{9,25},{17,1},{25,9},{2,18},{10... | collective-permute-start | bytes 49160 | tf_op jit(solution)/shard_map/ppermute | solution.py:655
  95.2 4.8 %collective-permute-start.28 = (f32[32,128]{1,0:T(8,128)S(1)}, f32[32,128]{1,0:T(8,128)S(1)}, u32[]{:S(2)}, u32[]{:S(2)}) collective-permute-start(f32[32,128]{1,0:T(8,128)S(1)} %pad_maximum_fusion.2), channel_id=1, source_target_pairs={{0,16},{8,24},{16,0},{24,8},{1,17},{9,25},{17,1},{25,9},{2,18},{10... | collective-permute-start | bytes 49160 | tf_op jit(solution)/shard_map/ppermute | solution.py:655
  (18 other events, 125.7 us)
where the time goes:
time: 113 us
  Pallas kernels  40.9 us (36%)
  waiting for transfers between devices  35.7 us (32%)
  starting transfers between devices  28.6 us (25%)
  local copies, waits for them, and re-layouts  4.99 us (4%)
  between operations  2.07 us (2%)
    pallas_call x14, Pallas kernels, kernel_call(): pl.pallas_call(kernel, out_shape=[jax.ShapeDtypeStruct(*one) for one in o...  40.9 us
    ppermute x9, waiting for transfers between devices, peers(): found.append(lax.ppermute(value, 'leaf', pairs))  22.7 us
    ppermute x9, starting transfers between devices, peers(): found.append(lax.ppermute(value, 'leaf', pairs))  17.2 us
    ppermute x6, waiting for transfers between devices, smooth_and_spread(): other = lax.ppermute(found, 'leaf', pairs)  8.46 us
    ppermute x6, starting transfers between devices, smooth_and_spread(): other = lax.ppermute(found, 'leaf', pairs)  4.82 us
    unnamed x20, local copies, waits for them, and re-layouts  4.28 us
    ppermute x3, waiting for transfers between devices, replicated(): traces.append(lax.ppermute(trace, 'probe', pairs))  3.9 us
    ppermute x3, starting transfers between devices, replicated(): traces.append(lax.ppermute(trace, 'probe', pairs))  3.49 us
  transfers between devices with their start and end apart: 32, of which 16 were waited for; matrix products, arithmetic and copies ran while one was open for 1% of the time, Pallas kernels for 23%

commit v1 on v0

--- a/solution.py
+++ b/solution.py
@@ -166,9 +166,10 @@
 
 
 class Dims:
-    def __init__(self, ndof, elem, parts, cap, modes, aggs):
+    def __init__(self, ndof, elem, parts, cap, modes, aggs, lines):
         self.ndof, self.elem, self.parts, self.cap = ndof, elem, parts, cap
         self.modes, self.aggs = modes, aggs
+        self.lines, self.share = lines, ndof // lines
         self.total = elem * parts
         self.half = parts // 2
         self.group = 2 * aggs
@@ -221,8 +222,8 @@
 
 
 def source_kernel(
-    dim, probe_in, sens_in, pairs_in, slots_in, agg_in, grad_in, trace_in, modes_in, inv_in,
-    visc_in, payload, sums, g3, gs, gsq3, my, m3t, trsq, inv,
+    dim, place, probe_in, sens_in, pairs_in, slots_in, agg_in, grad_in, trace_in, modes_in, inv_in,
+    visc_in, fric_in, weight_in, payload, quarter, sums, g3, gs, gsq3, my, m3t, trsq, inv,
     probe, sens, pairs, slots, agg_row, grad, trace, modes, sems,
 ):
     moves = (
@@ -235,7 +236,12 @@
         (trace_in, trace),
         (modes_in, modes),
         (inv_in, inv),
-        (visc_in, payload.at[pl.ds(dim.ndof + 8, dim.ndof)]),
+    )
+    share = dim.share
+    mine = pl.ds(pl.multiple_of(place[2] * share, share), share)
+    moves += tuple(
+        (field.at[mine], quarter.at[pl.ds(index * share, share)])
+        for index, field in enumerate((visc_in, fric_in, weight_in))
     )
     copies = [
         pltpu.make_async_copy(src, dst, sems.at[index]) for index, (src, dst) in enumerate(moves)
@@ -260,34 +266,38 @@
 
 
 def source_coarse_kernel(
-    dim, place, sums_own, sums_partner, inv_own, inv_partner, fric_in, out, sem
+    dim, place, payload, sums_own, sums_partner, inv_own, inv_partner, out
 ):
-    n = dim.ndof
-    copy = pltpu.make_async_copy(fric_in, out.at[pl.ds(0, n)], sem)
-    copy.start()
+    rows = dim.ndof + 8
     agg = place[1]
+    out[0:rows, :] = payload[...]
     sums = sums_own[...] + sums_partner[...]
     first, second = sums[:, 0 : dim.aggs], sums[:, dim.aggs :]
     mine = jnp.where(agg == 0, first, second)
     theirs = jnp.where(agg == 0, second, first)
-    out[pl.ds(pl.multiple_of(n + agg * dim.aggs, dim.aggs), dim.aggs), :] = solve_blocks(
+    out[pl.ds(pl.multiple_of(rows + agg * dim.aggs, dim.aggs), dim.aggs), :] = solve_blocks(
         mine, 0, inv_own, dim.aggs
     )
-    out[pl.ds(pl.multiple_of(n + (1 - agg) * dim.aggs, dim.aggs), dim.aggs), :] = solve_blocks(
+    out[pl.ds(pl.multiple_of(rows + (1 - agg) * dim.aggs, dim.aggs), dim.aggs), :] = solve_blocks(
         theirs, 0, inv_partner, dim.aggs
     )
-    copy.wait()
+
+
+def stack_kernel(*refs):
+    out = refs[-1]
+    rows = refs[0].shape[0]
+    for index, ref in enumerate(refs[:-1]):
+        out[index * rows : (index + 1) * rows, :] = ref[...]
 
 
 def build_kernel(dim, place, *refs):
     blocks = refs[: dim.parts]
-    source, visc, lap, hot2, counts, hot_own, table, sides, agg = refs[dim.parts :]
+    source, lap, hot2, counts, hot_own, table, sides, agg = refs[dim.parts :]
     n, e = dim.ndof, dim.elem
     for index, ref in enumerate(blocks):
         where = place[4 + index]
         columns = pl.ds(pl.multiple_of(where * e, e), e)
         source[:, columns] = ref[0:n, :]
-        visc[:, columns] = ref[n + 8 : 2 * n + 8, :]
         sides[pl.ds(where, 1), :] = ref[n : n + 1, :]
         sides[pl.ds(where + dim.parts, 1), :] = ref[n + 1 : n + 2, :]
         table[pl.ds(where, 1), :] = ref[n + 2 : n + 3, :]
@@ -419,9 +429,8 @@
 def gather_parts(dim, place, parts, solved):
     groups = []
     for ref in parts:
-        skip = ref.shape[0] % dim.ndof
-        first = ref.shape[0] - skip
-        groups += [(ref, first + step) for step in range(0, skip, dim.group)]
+        first = dim.ndof + 8 if ref.shape[0] > dim.ndof else 0
+        groups += [(ref, step) for step in range(first, ref.shape[0], dim.group)]
     for index, (ref, first) in enumerate(groups):
         where = place[4 + index] // 2
         solved[pl.ds(pl.multiple_of(where * dim.group, dim.group), dim.group), :] = ref[
@@ -429,13 +438,20 @@
         ]
 
 
-def begin_kernel(dim, place, source, visc, counts, trsq, lap, g3, gs, gsq3, *refs):
-    n, e = dim.ndof, dim.elem
-    fric_blocks = refs[: dim.parts]
-    fric, w_diag, smooth, v3, uy = refs[dim.parts :]
-    for index in range(dim.parts):
-        columns = pl.ds(pl.multiple_of(place[4 + index] * e, e), e)
-        fric[:, columns] = fric_blocks[index][0:n, :]
+def begin_kernel(dim, place, source, counts, trsq, lap, g3, gs, gsq3, *refs):
+    e = dim.elem
+    stacks = refs[: 2 * dim.lines]
+    visc, fric, weight, w_diag, smooth, v3, uy = refs[2 * dim.lines :]
+    share = dim.share
+    for index, ref in enumerate(stacks):
+        line = place[2] ^ (index % dim.lines)
+        rows = pl.ds(pl.multiple_of(line * share, share), share)
+        for chip in range(dim.half):
+            where = place[4 + chip + dim.half * (index // dim.lines)]
+            columns = pl.ds(pl.multiple_of(where * e, e), e)
+            for number, field in enumerate((visc, fric, weight)):
+                start = (3 * chip + number) * share
+                field[rows, columns] = ref[start : start + share, :]
     for c in chunks(dim):
         high, low = split(visc[:, c])
         diag = dot(gsq3[...], jnp.concatenate([high, low, high], axis=0))
@@ -459,11 +475,10 @@
 
 
 def middle_kernel(
-    dim, place, smooth, resid, search, scal, visc, fric, lap, g3, gs, hot2, my, m3t,
+    dim, place, smooth, resid, search, scal, weight, visc, fric, lap, g3, gs, hot2, my, m3t,
     hot_own, inv_own, inv_partner, *refs,
 ):
-    weights = refs[: dim.parts]
-    parts = refs[dim.parts : -8]
+    parts = refs[:-8]
     iterate, source, out, v3, uy, image, solved, precon = refs[-8:]
     e = dim.elem
     gather_parts(dim, place, parts, solved)
@@ -473,9 +488,7 @@
     second_step(dim, resid, search, precon, scal, consts, v3, uy, image)
     mine = pl.ds(pl.multiple_of(place[4] * e, e), e)
     iterate[...] = precon[:, mine]
-    for index, ref in enumerate(weights):
-        columns = pl.ds(pl.multiple_of(place[4 + index] * e, e), e)
-        source[:, columns] = ref[...] * precon[:, columns]
+    source[...] = weight[...] * precon[...]
     group_solve(dim, place, source, hot_own, m3t, inv_own, inv_partner, out)
 
 
@@ -531,6 +544,7 @@
         peer_slots.shape[2],
         coarse_modes.shape[1],
         coarse_inv.shape[0],
+        lax.axis_size("probe"),
     )
     n, e, ne = dim.ndof, dim.elem, dim.total
     leaf, agg = lax.axis_index("leaf"), lax.axis_index("agg")
@@ -538,7 +552,7 @@
     chips = leaf ^ order
     place = jnp.concatenate(
         [
-            jnp.stack([leaf, agg, leaf, agg]),
+            jnp.stack([leaf, agg, lax.axis_index("probe"), leaf]),
             chips * 2 + agg,
             chips * 2 + (1 - agg),
         ]
@@ -559,10 +573,11 @@
         own = peers(value)
         return own + [to_partner(one) for one in own]
 
-    payload, sums, g3, gs, gsq3, my, m3t, trsq, inv_own = call(
+    payload, quarter, sums, g3, gs, gsq3, my, m3t, trsq, inv_own = call(
         lambda *refs: source_kernel(dim, *refs),
         [
-            ((2 * n + 8, e), f32),
+            ((n + 8, e), f32),
+            ((3 * dim.share, e), f32),
             ((dim.modes, dim.group), f32),
             ((n, 3 * n), bf16),
             ((n, 6 * n), bf16),
@@ -572,9 +587,9 @@
             ((n, 1), f32),
             (coarse_inv.shape, f32),
         ],
-        [probes, sensitivity, local_pairs, peer_slots, elem_agg.reshape(1, e)]
-        + [grad_ref, trace_ref, coarse_modes, coarse_inv, viscosity],
-        [pltpu.HBM] * 10,
+        [place, probes, sensitivity, local_pairs, peer_slots, elem_agg.reshape(1, e)]
+        + [grad_ref, trace_ref, coarse_modes, coarse_inv, viscosity, friction, misfit_weight],
+        [SM] + [pltpu.HBM] * 12,
         scratch=[
             VM((n, e), f32),
             VM((n, e), f32),
@@ -584,30 +599,31 @@
             VM((n, n), f32),
             VM((n, n), f32),
             VM((n, dim.modes), f32),
-            pltpu.SemaphoreType.DMA((10,)),
+            pltpu.SemaphoreType.DMA((12,)),
         ],
         flops=10**8,
     )
-    source_blocks = gather(payload)
+    (stack,) = call(stack_kernel, [((3 * dim.share * dim.half, e), f32)], peers(quarter))
+    stacks = [stack]
+    for step in range(1, dim.lines):
+        pairs = [(index, index ^ step) for index in range(dim.lines)]
+        stacks.append(lax.ppermute(stack, "probe", pairs))
+    stacks += [to_partner(one) for one in stacks]
     inv_partner = to_partner(inv_own)
     sums_partner = to_partner(sums)
-    (second_payload,) = call(
+    (payload,) = call(
         lambda *refs: source_coarse_kernel(dim, *refs),
-        [((n + dim.group, e), f32)],
-        [place, sums, sums_partner, inv_own, inv_partner, friction],
-        [SM, VM, VM, VM, VM, pltpu.HBM],
-        scratch=[pltpu.SemaphoreType.DMA(())],
-    )
-    parts = peers(second_payload)
-    fric_blocks = parts + [to_partner(one) for one in parts]
-    own = peers(misfit_weight)
-    weight_blocks = own + [to_partner(one) for one in own]
+        [((n + 8 + dim.group, e), f32)],
+        [place, payload, sums, sums_partner, inv_own, inv_partner],
+        [SM, VM, VM, VM, VM, VM],
+    )
+    source_blocks = gather(payload)
+    parts = source_blocks[: dim.half]
 
     field = ((n, ne), f32)
-    source, visc, lap, hot2, counts, hot_own = call(
+    source, lap, hot2, counts, hot_own = call(
         lambda *refs: build_kernel(dim, *refs),
         [
-            field,
             field,
             ((ne, ne), bf16),
             ((dim.all_aggs, ne), bf16),
@@ -625,11 +641,11 @@
     out_shape = ((dim.group, dim.modes), f32)
     once = 2 * ne * n * (9 * n + 2 * ne)
 
-    fric, w_diag, smooth = call(
+    visc, fric, weight, w_diag, smooth = call(
         lambda *refs: begin_kernel(dim, *refs),
-        [field] * 3,
-        [place, source, visc, counts, trsq, lap, g3, gs, gsq3] + fric_blocks,
-        [SM] + [VM] * (8 + dim.parts),
+        [field] * 5,
+        [place, source, counts, trsq, lap, g3, gs, gsq3] + stacks,
+        [SM] + [VM] * (7 + len(stacks)),
         scratch=work,
         flops=2 * once,
     )
@@ -676,11 +692,10 @@
     iterate, source_two, out = call(
         lambda *refs: middle_kernel(dim, *refs),
         [((n, e), f32), field, out_shape],
-        [place, smooth, resid, search, scal, visc, fric, lap, g3, gs, hot2, my]
+        [place, smooth, resid, search, scal, weight, visc, fric, lap, g3, gs, hot2, my]
         + [m3t, hot_own, inv_own, inv_partner]
-        + weight_blocks
         + parts,
-        [SM] + [VM] * (15 + dim.parts + len(parts)),
+        [SM] + [VM] * (16 + len(parts)),
         scratch=work + [image, solved, image],
         flops=once,
     )
@@ -709,7 +724,7 @@
 
 
 def fits_one_core(mesh, viscosity, coarse_modes, coarse_inv, peer_slots, local_pairs):
-    leaf_count, agg_count = mesh.shape["leaf"], mesh.shape["agg"]
+    leaf_count, agg_count, probe_count = (mesh.shape[name] for name in ("leaf", "agg", "probe"))
     ndof, elem = viscosity.shape
     parts = leaf_count * agg_count
     cap = peer_slots.shape[2]
@@ -723,6 +738,8 @@
         and parts * cap == elem
         and local_pairs.shape[1] == elem
         and ndof % 16 == 0
+        and ndof % (8 * probe_count) == 0
+        and probe_count & (probe_count - 1) == 0
         and aggs % 8 == 0
         and local_pairs.shape[1] + (parts - 1) * cap <= 256
         and parts * elem <= 1024

time: 113 us -> 98.6 us (0.87)
  waiting for transfers between devices: 35.7 us -> 29.5 us
  local copies, waits for them, and re-layouts: 4.99 us -> 0.09 us
  starting transfers between devices: 28.6 us -> 26 us
    ppermute x9 -> x6, waiting for transfers between devices: 22.7 us -> 9.68 us  [peers(): found.append(lax.ppermute(value, 'leaf', pairs))]
    ppermute x9 -> x6, starting transfers between devices: 17.2 us -> 9.8 us  [peers(): found.append(lax.ppermute(value, 'leaf', pairs))]
    ppermute x0 -> x3, waiting for transfers between devices: none -> 6.49 us  [replicated(): stacks.append(lax.ppermute(stack, 'probe', pairs))]
    unnamed x20 -> x2, local copies, waits for them, and re-layouts: 4.28 us -> 0.01 us
    ppermute x0 -> x3, starting transfers between devices: none -> 3.55 us  [replicated(): stacks.append(lax.ppermute(stack, 'probe', pairs))]
    ppermute x6, waiting for transfers between devices: 8.46 us -> 5.38 us  [smooth_and_spread(): other = lax.ppermute(found, 'leaf', pairs)]
    ppermute x14 -> x10, waiting for transfers between devices: 0.66 us -> 3.68 us  [to_partner(): return lax.ppermute(value, 'agg', flip)]
    ppermute x6, starting transfers between devices: 4.82 us -> 7.32 us  [smooth_and_spread(): other = lax.ppermute(found, 'leaf', pairs)]
  transfers between devices with their start and end apart: 32 -> 28, of which waited for: 16 -> 18; matrix products, arithmetic and copies ran while one was open for 1% -> 0% of each run, Pallas kernels for 23% -> 16%
where the time goes in v1:
time: 98.6 us; the launch traced here: 98.4 us
  Pallas kernels  40.8 us (41%)
  waiting for transfers between devices  29.5 us (30%)
  starting transfers between devices  26 us (26%)
  between operations  2.04 us (2%)
    pallas_call x15, Pallas kernels, kernel_call(): pl.pallas_call(kernel, out_shape=[jax.ShapeDtypeStruct(*one) for one in o...  40.8 us
    ppermute x6, starting transfers between devices, peers(): found.append(lax.ppermute(value, 'leaf', pairs))  9.8 us
    ppermute x6, waiting for transfers between devices, peers(): found.append(lax.ppermute(value, 'leaf', pairs))  9.68 us
    ppermute x6, starting transfers between devices, smooth_and_spread(): other = lax.ppermute(found, 'leaf', pairs)  7.32 us
    ppermute x3, waiting for transfers between devices, replicated(): stacks.append(lax.ppermute(stack, 'probe', pairs))  6.49 us
    ppermute x6, waiting for transfers between devices, smooth_and_spread(): other = lax.ppermute(found, 'leaf', pairs)  5.38 us
    ppermute x3, waiting for transfers between devices, replicated(): traces.append(lax.ppermute(trace, 'probe', pairs))  4.29 us
    ppermute x10, waiting for transfers between devices, to_partner(): return lax.ppermute(value, 'agg', flip)  3.68 us
  transfers between devices with their start and end apart: 28, of which 18 were waited for; matrix products, arithmetic and copies ran while one was open for 0% of the time, Pallas kernels for 16%

profile of v1, /device:TPU:0, one launch (start us, length us, event | category | flops | bytes accessed | tf_op | source)
XLA Modules:
  0.0 98.4 jit_solution(13909626883664550613)
XLA Ops:
  0.7 2.7 %shard_map.139 = (f32[200,128]{1,0:T(8,128)S(1)}, f32[144,128]{1,0:T(8,128)S(1)}, f32[128,16]{1,0:T(8,128)S(1)}, bf16[192,576]{1,0:T(8,128)(2,1)S(1)}, bf16[192,...) custom-call(s32[12]{0:T(128)S(1)} %concatenate.12.refs_0_, ...), custom_call_target="tpu_custom_call" | custom-call | flops 100000000 | tf_op jit(solution)/shard_map/pallas_call | solution.py:155
  4.0 4.7 %collective-permute-start.11 = (f32[144,128]{1,0:T(8,128)S(1)}, f32[144,128]{1,0:T(8,128)S(1)}, u32[]{:S(2)}, u32[]{:S(2)}) collective-permute-start(f32[144,128]{1,0:T(8,128)S(1)} %get-tuple-element.46.refs_0_), channel_id=1, source_target_pairs={{0,24},{8,16},{16,8},{24,0},{1,25},{9,17},{17,9},{25,1},{2,26},{10... | collective-permute-start | bytes 221192 | tf_op jit(solution)/shard_map/ppermute | solution.py:569
  9.3 2.6 %collective-permute-done.11.refs_3_ = f32[144,128]{1,0:T(8,128)S(1)} collective-permute-done((f32[144,128]{1,0:T(8,128)S(1)}, f32[144,128]{1,0:T(8,128)S(1)}, u32[]{:S(2)}, u32[]{:S(2)}) %collective-permute-start.11) | collective-permute-done | bytes 73760 | tf_op jit(solution)/shard_map/ppermute | solution.py:569
  11.9 3.5 %collective-permute-done.10.refs_2_ = f32[144,128]{1,0:T(8,128)S(1)} collective-permute-done((f32[144,128]{1,0:T(8,128)S(1)}, f32[144,128]{1,0:T(8,128)S(1)}, u32[]{:S(2)}, u32[]{:S(2)}) %collective-permute-start.10) | collective-permute-done | bytes 73760 | tf_op jit(solution)/shard_map/ppermute | solution.py:569
  15.4 2.5 %collective-permute-start.14 = (f32[576,128]{1,0:T(8,128)S(1)}, f32[576,128]{1,0:T(8,128)S(1)}, u32[]{:S(2)}, u32[]{:S(2)}) collective-permute-start(f32[576,128]{1,0:T(8,128)S(1)} %shard_map.142.refs_8_), channel_id=1, source_target_pairs={{0,3},{1,2},{2,1},{3,0},{4,7},{5,6},{6,5},{7,4},{8,11},{9,10},{10,... | collective-permute-start | bytes 884744 | tf_op jit(solution)/shard_map/ppermute | solution.py:610
  21.3 2.5 %collective-permute-start.4 = (f32[216,128]{1,0:T(8,128)S(1)}, f32[216,128]{1,0:T(8,128)S(1)}, u32[]{:S(2)}, u32[]{:S(2)}) collective-permute-start(f32[216,128]{1,0:T(8,128)S(1)} %shard_map.140.refs_1_.refs_14_), channel_id=1, source_target_pairs={{0,24},{8,16},{16,8},{24,0},{1,25},{9,17},{17,9},{25,1},{2,26},{10... | collective-permute-start | bytes 331784 | tf_op jit(solution)/shard_map/ppermute | solution.py:569
  23.8 2.5 %collective-permute-done.14.refs_11_ = f32[576,128]{1,0:T(8,128)S(1)} collective-permute-done((f32[576,128]{1,0:T(8,128)S(1)}, f32[576,128]{1,0:T(8,128)S(1)}, u32[]{:S(2)}, u32[]{:S(2)}) %collective-permute-start.14) | collective-permute-done | bytes 294944 | tf_op jit(solution)/shard_map/ppermute | solution.py:610
  27.2 4.0 %collective-permute-done.13.refs_10_ = f32[576,128]{1,0:T(8,128)S(1)} collective-permute-done((f32[576,128]{1,0:T(8,128)S(1)}, f32[576,128]{1,0:T(8,128)S(1)}, u32[]{:S(2)}, u32[]{:S(2)}) %collective-permute-start.13) | collective-permute-done | bytes 294944 | tf_op jit(solution)/shard_map/ppermute | solution.py:610
  34.1 2.3 %collective-permute-done.2.refs_2_.refs_15_ = f32[216,128]{1,0:T(8,128)S(1)} collective-permute-done((f32[216,128]{1,0:T(8,128)S(1)}, f32[216,128]{1,0:T(8,128)S(1)}, u32[]{:S(2)}, u32[]{:S(2)}) %collective-permute-start.2) | collective-permute-done | bytes 110624 | tf_op jit(solution)/shard_map/ppermute | solution.py:569
  39.5 2.3 %shard_map.141 = (f32[192,1024]{1,0:T(8,128)S(1)}, bf16[1024,1024]{1,0:T(8,128)(2,1)S(1)}, bf16[64,1024]{1,0:T(8,128)(2,1)S(1)}, f32[1,1024]{1,0:T(1,128)S(1)}, bf16[16,256]{1,0:T(8,128)(2,1)S(1)}) custom-call(s32[12]{0:T(128)S(1)} %concatenate.12.refs_0_, f32[216,128]{1,0:T(8,128)S(1)} %shard_map.140.refs_1_.refs_14_, ...), custom_call_target="tpu_custom_call" | custom-call | tf_op jit(solution)/shard_map/pallas_call | solution.py:155
  41.9 5.4 %shard_map.143 = (f32[192,1024]{1,0:T(8,128)S(1)}, f32[192,1024]{1,0:T(8,128)S(1)}, f32[192,1024]{1,0:T(8,128)S(1)}, f32[192,1024]{1,0:T(8,128)S(1)}, f32[192,1024]{1,0:T(8,128)S(1)}) custom-call(s32[12]{0:T(128)S(1)} %concatenate.12.refs_0_, f32[192,1024]{1,0:T(8,128)S(1)} %get-tuple-element.39.refs_1_.refs_2_.refs_5_, ...), custom_call_target="tpu_custom_call" | custom-call | flops 2969567232 | tf_op jit(solution)/shard_map/pallas_call | solution.py:155
  47.3 4.0 %shard_map.144 = (f32[192,1024]{1,0:T(8,128)S(1)}, f32[192,1024]{1,0:T(8,128)S(1)}, f32[8,128]{1,0:T(8,128)S(1)}, f32[16,128]{1,0:T(8,128)S(1)}) custom-call(s32[12]{0:T(128)S(1)} %concatenate.12.refs_0_, f32[192,1024]{1,0:T(8,128)S(1)} %get-tuple-element.47.refs_1_, f32[192,1024]{1,0:T(8,128)S(1)} %get-tuple-element.39.refs_1_.refs_2_.refs_5_, ...), custom_call_target="tpu_custom_call" | custom-call | flops 1484783616 | tf_op jit(solution)/shard_map/pallas_call | solution.py:155
  52.2 2.1 %shard_map.145.refs_7_ = f32[192,1024]{1,0:T(8,128)S(1)} custom-call(f32[192,1024]{1,0:T(8,128)S(1)} %get-tuple-element.54.refs_0_.refs_2_, f32[192,1024]{1,0:T(8,128)S(1)} %get-tuple-element.48.refs_3_.refs_1_.refs_6_.refs_7_, f32[192,1024]{1,0:T(8,128)S(1)} %get-tuple-element.49.refs_4_.refs_2_.refs_7_.refs_8_, f32[192,1024]{1,0:T(8,128)S(1)} %get-tuple-element.55.refs_3_, ...), custom_call_target="tpu_custom_call" | custom-call | flops 1484783616 | tf_op jit(solution)/shard_map/pallas_call | solution.py:155
  56.4 2.0 %shard_map.146.refs_1_ = f32[192,1024]{1,0:T(8,128)S(1)} custom-call(f32[192,1024]{1,0:T(8,128)S(1)} %get-tuple-element.54.refs_0_.refs_2_, f32[192,1024]{1,0:T(8,128)S(1)} %get-tuple-element.48.refs_3_.refs_1_.refs_6_.refs_7_, f32[192,1024]{1,0:T(8,128)S(1)} %get-tuple-element.49.refs_4_.refs_2_.refs_7_.refs_8_, f32[192,1024]{1,0:T(8,128)S(1)} %get-tuple-element.55.refs_3_, ...), custom_call_target="tpu_custom_call" | custom-call | flops 1484783616 | tf_op jit(solution)/shard_map/pallas_call | solution.py:155
  59.7 4.4 %shard_map.147 = (f32[192,128]{1,0:T(8,128)}, f32[192,1024]{1,0:T(8,128)S(1)}, f32[16,128]{1,0:T(8,128)S(1)}) custom-call(s32[12]{0:T(128)S(1)} %concatenate.12.refs_0_, f32[192,1024]{1,0:T(8,128)S(1)} %shard_map.146.refs_1_, f32[192,1024]{1,0:T(8,128)S(1)} %get-tuple-element.54.refs_0_.refs_2_, f32[192,1024]{1,0:T(8,128)S(1)} %get-tuple-element.56.refs_3_, ...), custom_call_target="tpu_custom_call" | custom-call | flops 1484783616 | tf_op jit(solution)/shard_map/pallas_call | solution.py:155
  65.0 2.1 %shard_map.148.refs_7_ = f32[192,1024]{1,0:T(8,128)S(1)} custom-call(f32[192,1024]{1,0:T(8,128)S(1)} %get-tuple-element.61.refs_0_.refs_2_, f32[192,1024]{1,0:T(8,128)S(1)} %get-tuple-element.48.refs_3_.refs_1_.refs_6_.refs_7_, f32[192,1024]{1,0:T(8,128)S(1)} %get-tuple-element.49.refs_4_.refs_2_.refs_7_.refs_8_, f32[192,1024]{1,0:T(8,128)S(1)} %get-tuple-element.55.refs_3_, ...), custom_call_target="tpu_custom_call" | custom-call | flops 1484783616 | tf_op jit(solution)/shard_map/pallas_call | solution.py:155
  69.4 2.0 %shard_map.149.refs_1_ = f32[192,1024]{1,0:T(8,128)S(1)} custom-call(f32[192,1024]{1,0:T(8,128)S(1)} %get-tuple-element.61.refs_0_.refs_2_, f32[192,1024]{1,0:T(8,128)S(1)} %get-tuple-element.48.refs_3_.refs_1_.refs_6_.refs_7_, f32[192,1024]{1,0:T(8,128)S(1)} %get-tuple-element.49.refs_4_.refs_2_.refs_7_.refs_8_, f32[192,1024]{1,0:T(8,128)S(1)} %get-tuple-element.55.refs_3_, ...), custom_call_target="tpu_custom_call" | custom-call | flops 1484783616 | tf_op jit(solution)/shard_map/pallas_call | solution.py:155
  72.5 4.3 %shard_map.150 = (f32[192,1024]{1,0:T(8,128)S(1)}, f32[192,1024]{1,0:T(8,128)S(1)}, f32[8,128]{1,0:T(8,128)S(1)}, f32[16,128]{1,0:T(8,128)S(1)}) custom-call(s32[12]{0:T(128)S(1)} %concatenate.12.refs_0_, f32[192,1024]{1,0:T(8,128)S(1)} %shard_map.149.refs_1_, f32[192,1024]{1,0:T(8,128)S(1)} %get-tuple-element.61.refs_0_.refs_2_, ...), custom_call_target="tpu_custom_call" | custom-call | flops 1484783616 | tf_op jit(solution)/shard_map/pallas_call | solution.py:155
  77.7 2.1 %shard_map.151.refs_7_ = f32[192,1024]{1,0:T(8,128)S(1)} custom-call(f32[192,1024]{1,0:T(8,128)S(1)} %get-tuple-element.63.refs_0_.refs_2_, f32[192,1024]{1,0:T(8,128)S(1)} %get-tuple-element.48.refs_3_.refs_1_.refs_6_.refs_7_, f32[192,1024]{1,0:T(8,128)S(1)} %get-tuple-element.49.refs_4_.refs_2_.refs_7_.refs_8_, f32[192,1024]{1,0:T(8,128)S(1)} %get-tuple-element.55.refs_3_, ...), custom_call_target="tpu_custom_call" | custom-call | flops 1484783616 | tf_op jit(solution)/shard_map/pallas_call | solution.py:155
  80.5 1.7 %collective-permute-start.24 = (f32[32,128]{1,0:T(8,128)S(1)}, f32[32,128]{1,0:T(8,128)S(1)}, u32[]{:S(2)}, u32[]{:S(2)}) collective-permute-start(f32[32,128]{1,0:T(8,128)S(1)} %pad_maximum_fusion.2), channel_id=1, source_target_pairs={{0,16},{8,24},{16,0},{24,8},{1,17},{9,25},{17,1},{25,9},{2,18},{10... | collective-permute-start | bytes 49160 | tf_op jit(solution)/shard_map/ppermute | solution.py:671
  82.2 2.0 %shard_map.152.refs_1_ = f32[192,1024]{1,0:T(8,128)S(1)} custom-call(f32[192,1024]{1,0:T(8,128)S(1)} %get-tuple-element.63.refs_0_.refs_2_, f32[192,1024]{1,0:T(8,128)S(1)} %get-tuple-element.48.refs_3_.refs_1_.refs_6_.refs_7_, f32[192,1024]{1,0:T(8,128)S(1)} %get-tuple-element.49.refs_4_.refs_2_.refs_7_.refs_8_, f32[192,1024]{1,0:T(8,128)S(1)} %get-tuple-element.55.refs_3_, ...), custom_call_target="tpu_custom_call" | custom-call | flops 1484783616 | tf_op jit(solution)/shard_map/pallas_call | solution.py:155
  85.1 4.3 %shard_map.153 = (f32[192,128]{1,0:T(8,128)}, f32[1,128]{1,0:T(1,128)S(1)}) custom-call(s32[12]{0:T(128)S(1)} %concatenate.12.refs_0_, f32[192,1024]{1,0:T(8,128)S(1)} %shard_map.152.refs_1_, f32[192,1024]{1,0:T(8,128)S(1)} %get-tuple-element.63.refs_0_.refs_2_, f32[192,1024]{1,0:T(8,128)S(1)} %get-tuple-element.64.refs_3_, ...), custom_call_target="tpu_custom_call" | custom-call | flops 1484783616 | tf_op jit(solution)/shard_map/pallas_call | solution.py:155
  90.9 1.9 %collective-permute-start.26 = (f32[1,128]{1,0:T(1,128)S(1)}, f32[1,128]{1,0:T(1,128)S(1)}, u32[]{:S(2)}, u32[]{:S(2)}) collective-permute-start(f32[1,128]{1,0:T(1,128)S(1)} %get-tuple-element.68), channel_id=1, source_target_pairs={{0,2},{1,3},{2,0},{3,1},{4,6},{5,7},{6,4},{7,5},{8,10},{9,11},{10,... | collective-permute-start | bytes 1544 | tf_op jit(solution)/shard_map/ppermute | solution.py:721
  94.5 2.8 %collective-permute-done.27 = f32[1,128]{1,0:T(1,128)S(1)} collective-permute-done((f32[1,128]{1,0:T(1,128)S(1)}, f32[1,128]{1,0:T(1,128)S(1)}, u32[]{:S(2)}, u32[]{:S(2)}) %collective-permute-start.27) | collective-permute-done | bytes 544 | tf_op jit(solution)/shard_map/ppermute | solution.py:721
  (54 shorter events, 25.6 us)
Async XLA Ops:
  3.4 16.8 %collective-permute-start.1 = (f32[8,128,128]{2,1,0:T(8,128)S(1)}, f32[8,128,128]{2,1,0:T(8,128)S(1)}, u32[]{:S(2)}, u32[]{:S(2)}) collective-permute-start(f32[8,128,128]{2,1,0:T(8,128)S(1)} %get-tuple-element.38.refs_4_.refs_12_.refs_15_), channel_id=1, source_target_pairs={{0,4},{4,0},{1,5},{5,1},{2,6},{6,2},{3,7},{7,3},{8,12},{12,8},{9,1... | collective-permute-start | bytes 1572872 | tf_op jit(solution)/shard_map/ppermute | solution.py:563
  4.0 7.9 %collective-permute-start.11 = (f32[144,128]{1,0:T(8,128)S(1)}, f32[144,128]{1,0:T(8,128)S(1)}, u32[]{:S(2)}, u32[]{:S(2)}) collective-permute-start(f32[144,128]{1,0:T(8,128)S(1)} %get-tuple-element.46.refs_0_), channel_id=1, source_target_pairs={{0,24},{8,16},{16,8},{24,0},{1,25},{9,17},{17,9},{25,1},{2,26},{10... | collective-permute-start | bytes 221192 | tf_op jit(solution)/shard_map/ppermute | solution.py:569
  8.7 6.8 %collective-permute-start.10 = (f32[144,128]{1,0:T(8,128)S(1)}, f32[144,128]{1,0:T(8,128)S(1)}, u32[]{:S(2)}, u32[]{:S(2)}) collective-permute-start(f32[144,128]{1,0:T(8,128)S(1)} %get-tuple-element.46.refs_0_), channel_id=1, source_target_pairs={{0,16},{8,24},{16,0},{24,8},{1,17},{9,25},{17,1},{25,9},{2,18},{10... | collective-permute-start | bytes 221192 | tf_op jit(solution)/shard_map/ppermute | solution.py:569
  8.7 6.8 %collective-permute-start.9 = (f32[144,128]{1,0:T(8,128)S(1)}, f32[144,128]{1,0:T(8,128)S(1)}, u32[]{:S(2)}, u32[]{:S(2)}) collective-permute-start(f32[144,128]{1,0:T(8,128)S(1)} %get-tuple-element.46.refs_0_), channel_id=1, source_target_pairs={{0,8},{8,0},{16,24},{24,16},{1,9},{9,1},{17,25},{25,17},{2,10},{10... | collective-permute-start | bytes 221192 | tf_op jit(solution)/shard_map/ppermute | solution.py:569
  15.4 10.9 %collective-permute-start.14 = (f32[576,128]{1,0:T(8,128)S(1)}, f32[576,128]{1,0:T(8,128)S(1)}, u32[]{:S(2)}, u32[]{:S(2)}) collective-permute-start(f32[576,128]{1,0:T(8,128)S(1)} %shard_map.142.refs_8_), channel_id=1, source_target_pairs={{0,3},{1,2},{2,1},{3,0},{4,7},{5,6},{6,5},{7,4},{8,11},{9,10},{10,... | collective-permute-start | bytes 884744 | tf_op jit(solution)/shard_map/ppermute | solution.py:610
  18.0 13.3 %collective-permute-start.13 = (f32[576,128]{1,0:T(8,128)S(1)}, f32[576,128]{1,0:T(8,128)S(1)}, u32[]{:S(2)}, u32[]{:S(2)}) collective-permute-start(f32[576,128]{1,0:T(8,128)S(1)} %shard_map.142.refs_8_), channel_id=1, source_target_pairs={{0,2},{1,3},{2,0},{3,1},{4,6},{5,7},{6,4},{7,5},{8,10},{9,11},{10,... | collective-permute-start | bytes 884744 | tf_op jit(solution)/shard_map/ppermute | solution.py:610
  18.5 13.8 %collective-permute-start.12 = (f32[576,128]{1,0:T(8,128)S(1)}, f32[576,128]{1,0:T(8,128)S(1)}, u32[]{:S(2)}, u32[]{:S(2)}) collective-permute-start(f32[576,128]{1,0:T(8,128)S(1)} %shard_map.142.refs_8_), channel_id=1, source_target_pairs={{0,1},{1,0},{2,3},{3,2},{4,5},{5,4},{6,7},{7,6},{8,9},{9,8},{10,11... | collective-permute-start | bytes 884744 | tf_op jit(solution)/shard_map/ppermute | solution.py:610
  21.3 11.0 %collective-permute-start.4 = (f32[216,128]{1,0:T(8,128)S(1)}, f32[216,128]{1,0:T(8,128)S(1)}, u32[]{:S(2)}, u32[]{:S(2)}) collective-permute-start(f32[216,128]{1,0:T(8,128)S(1)} %shard_map.140.refs_1_.refs_14_), channel_id=1, source_target_pairs={{0,24},{8,16},{16,8},{24,0},{1,25},{9,17},{17,9},{25,1},{2,26},{10... | collective-permute-start | bytes 331784 | tf_op jit(solution)/shard_map/ppermute | solution.py:569
  23.8 9.0 %collective-permute-start.5 = (f32[216,128]{1,0:T(8,128)S(1)}, f32[216,128]{1,0:T(8,128)S(1)}, u32[]{:S(2)}, u32[]{:S(2)}) collective-permute-start(f32[216,128]{1,0:T(8,128)S(1)} %shard_map.140.refs_1_.refs_14_), channel_id=1, source_target_pairs={{0,4},{4,0},{1,5},{5,1},{2,6},{6,2},{3,7},{7,3},{8,12},{12,8},{9,1... | collective-permute-start | bytes 331784 | tf_op jit(solution)/shard_map/ppermute | solution.py:563
  26.3 7.7 %collective-permute-start.3 = (f32[216,128]{1,0:T(8,128)S(1)}, f32[216,128]{1,0:T(8,128)S(1)}, u32[]{:S(2)}, u32[]{:S(2)}) collective-permute-start(f32[216,128]{1,0:T(8,128)S(1)} %shard_map.140.refs_1_.refs_14_), channel_id=1, source_target_pairs={{0,16},{8,24},{16,0},{24,8},{1,17},{9,25},{17,1},{25,9},{2,18},{10... | collective-permute-start | bytes 331784 | tf_op jit(solution)/shard_map/ppermute | solution.py:569
  31.2 5.2 %collective-permute-start.2 = (f32[216,128]{1,0:T(8,128)S(1)}, f32[216,128]{1,0:T(8,128)S(1)}, u32[]{:S(2)}, u32[]{:S(2)}) collective-permute-start(f32[216,128]{1,0:T(8,128)S(1)} %shard_map.140.refs_1_.refs_14_), channel_id=1, source_target_pairs={{0,8},{8,0},{16,24},{24,16},{1,9},{9,1},{17,25},{25,17},{2,10},{10... | collective-permute-start | bytes 331784 | tf_op jit(solution)/shard_map/ppermute | solution.py:569
  32.3 4.2 %collective-permute-start.8 = (f32[216,128]{1,0:T(8,128)S(1)}, f32[216,128]{1,0:T(8,128)S(1)}, u32[]{:S(2)}, u32[]{:S(2)}) collective-permute-start(f32[216,128]{1,0:T(8,128)S(1)} %collective-permute-done.4.refs_4_.refs_17_), channel_id=1, source_target_pairs={{0,4},{4,0},{1,5},{5,1},{2,6},{6,2},{3,7},{7,3},{8,12},{12,8},{9,1... | collective-permute-start | bytes 331784 | tf_op jit(solution)/shard_map/ppermute | solution.py:563
  32.3 9.6 %collective-permute-start.15 = (f32[576,128]{1,0:T(8,128)S(1)}, f32[576,128]{1,0:T(8,128)S(1)}, u32[]{:S(2)}, u32[]{:S(2)}) collective-permute-start(f32[576,128]{1,0:T(8,128)S(1)} %shard_map.142.refs_8_), channel_id=1, source_target_pairs={{0,4},{4,0},{1,5},{5,1},{2,6},{6,2},{3,7},{7,3},{8,12},{12,8},{9,1... | collective-permute-start | bytes 884744 | tf_op jit(solution)/shard_map/ppermute | solution.py:563
  32.8 9.1 %collective-permute-start.18 = (f32[576,128]{1,0:T(8,128)S(1)}, f32[576,128]{1,0:T(8,128)S(1)}, u32[]{:S(2)}, u32[]{:S(2)}) collective-permute-start(f32[576,128]{1,0:T(8,128)S(1)} %collective-permute-done.14.refs_11_), channel_id=1, source_target_pairs={{0,4},{4,0},{1,5},{5,1},{2,6},{6,2},{3,7},{7,3},{8,12},{12,8},{9,1... | collective-permute-start | bytes 884744 | tf_op jit(solution)/shard_map/ppermute | solution.py:563
  34.1 7.8 %collective-permute-start.17 = (f32[576,128]{1,0:T(8,128)S(1)}, f32[576,128]{1,0:T(8,128)S(1)}, u32[]{:S(2)}, u32[]{:S(2)}) collective-permute-start(f32[576,128]{1,0:T(8,128)S(1)} %collective-permute-done.13.refs_10_), channel_id=1, source_target_pairs={{0,4},{4,0},{1,5},{5,1},{2,6},{6,2},{3,7},{7,3},{8,12},{12,8},{9,1... | collective-permute-start | bytes 884744 | tf_op jit(solution)/shard_map/ppermute | solution.py:563
  36.4 5.4 %collective-permute-start.16 = (f32[576,128]{1,0:T(8,128)S(1)}, f32[576,128]{1,0:T(8,128)S(1)}, u32[]{:S(2)}, u32[]{:S(2)}) collective-permute-start(f32[576,128]{1,0:T(8,128)S(1)} %collective-permute-done.12.refs_9_), channel_id=1, source_target_pairs={{0,4},{4,0},{1,5},{5,1},{2,6},{6,2},{3,7},{7,3},{8,12},{12,8},{9,1... | collective-permute-start | bytes 884744 | tf_op jit(solution)/shard_map/ppermute | solution.py:563
  51.3 3.7 %collective-permute-start.19 = (f32[16,128]{1,0:T(8,128)S(1)}, f32[16,128]{1,0:T(8,128)S(1)}, u32[]{:S(2)}, u32[]{:S(2)}) collective-permute-start(f32[16,128]{1,0:T(8,128)S(1)} %get-tuple-element.59.refs_17_), channel_id=1, source_target_pairs={{0,8},{8,0},{16,24},{24,16},{1,9},{9,1},{17,25},{25,17},{2,10},{10... | collective-permute-start | bytes 24584 | tf_op jit(solution)/shard_map/ppermute | solution.py:671
  55.1 4.6 %collective-permute-start.20 = (f32[32,128]{1,0:T(8,128)S(1)}, f32[32,128]{1,0:T(8,128)S(1)}, u32[]{:S(2)}, u32[]{:S(2)}) collective-permute-start(f32[32,128]{1,0:T(8,128)S(1)} %pad_maximum_fusion), channel_id=1, source_target_pairs={{0,16},{8,24},{16,0},{24,8},{1,17},{9,25},{17,1},{25,9},{2,18},{10... | collective-permute-start | bytes 49160 | tf_op jit(solution)/shard_map/ppermute | solution.py:671
  64.1 3.7 %collective-permute-start.21 = (f32[16,128]{1,0:T(8,128)S(1)}, f32[16,128]{1,0:T(8,128)S(1)}, u32[]{:S(2)}, u32[]{:S(2)}) collective-permute-start(f32[16,128]{1,0:T(8,128)S(1)} %get-tuple-element.62.refs_14_), channel_id=1, source_target_pairs={{0,8},{8,0},{16,24},{24,16},{1,9},{9,1},{17,25},{25,17},{2,10},{10... | collective-permute-start | bytes 24584 | tf_op jit(solution)/shard_map/ppermute | solution.py:671
  67.9 4.6 %collective-permute-start.22 = (f32[32,128]{1,0:T(8,128)S(1)}, f32[32,128]{1,0:T(8,128)S(1)}, u32[]{:S(2)}, u32[]{:S(2)}) collective-permute-start(f32[32,128]{1,0:T(8,128)S(1)} %pad_maximum_fusion.1), channel_id=1, source_target_pairs={{0,16},{8,24},{16,0},{24,8},{1,17},{9,25},{17,1},{25,9},{2,18},{10... | collective-permute-start | bytes 49160 | tf_op jit(solution)/shard_map/ppermute | solution.py:671
  76.8 3.7 %collective-permute-start.23 = (f32[16,128]{1,0:T(8,128)S(1)}, f32[16,128]{1,0:T(8,128)S(1)}, u32[]{:S(2)}, u32[]{:S(2)}) collective-permute-start(f32[16,128]{1,0:T(8,128)S(1)} %get-tuple-element.66.refs_14_), channel_id=1, source_target_pairs={{0,8},{8,0},{16,24},{24,16},{1,9},{9,1},{17,25},{25,17},{2,10},{10... | collective-permute-start | bytes 24584 | tf_op jit(solution)/shard_map/ppermute | solution.py:671
  80.5 4.6 %collective-permute-start.24 = (f32[32,128]{1,0:T(8,128)S(1)}, f32[32,128]{1,0:T(8,128)S(1)}, u32[]{:S(2)}, u32[]{:S(2)}) collective-permute-start(f32[32,128]{1,0:T(8,128)S(1)} %pad_maximum_fusion.2), channel_id=1, source_target_pairs={{0,16},{8,24},{16,0},{24,8},{1,17},{9,25},{17,1},{25,9},{2,18},{10... | collective-permute-start | bytes 49160 | tf_op jit(solution)/shard_map/ppermute | solution.py:671
  89.4 3.6 %collective-permute-start.25 = (f32[1,128]{1,0:T(1,128)S(1)}, f32[1,128]{1,0:T(1,128)S(1)}, u32[]{:S(2)}, u32[]{:S(2)}) collective-permute-start(f32[1,128]{1,0:T(1,128)S(1)} %get-tuple-element.68), channel_id=1, source_target_pairs={{0,1},{1,0},{2,3},{3,2},{4,5},{5,4},{6,7},{7,6},{8,9},{9,8},{10,11... | collective-permute-start | bytes 1544 | tf_op jit(solution)/shard_map/ppermute | solution.py:721
  92.8 4.5 %collective-permute-start.27 = (f32[1,128]{1,0:T(1,128)S(1)}, f32[1,128]{1,0:T(1,128)S(1)}, u32[]{:S(2)}, u32[]{:S(2)}) collective-permute-start(f32[1,128]{1,0:T(1,128)S(1)} %get-tuple-element.68), channel_id=1, source_target_pairs={{0,3},{1,2},{2,1},{3,0},{4,7},{5,6},{6,5},{7,4},{8,11},{9,10},{10,... | collective-permute-start | bytes 1544 | tf_op jit(solution)/shard_map/ppermute | solution.py:721
  (5 other events, 12.5 us)

commit v2 on v1

--- a/solution.py
+++ b/solution.py
@@ -380,62 +380,46 @@
     lax.fori_loop(0, SWEEPS - 1, sweep, 0)
 
 
-def coarse_add(dim, solved, my, hot2, target):
+def coarse_add(dim, solved, my, hot2, base, target):
     high, low = split(solved)
     coarse = dot_nt(my[...], jnp.concatenate([high, low, high], axis=1))
     high, low = split(coarse)
     for c in chunks(dim):
-        target[:, c] = target[:, c] + dot(high, hot2[:, c]) + dot(low, hot2[:, c])
-
-
-def group_solve(dim, place, resid, hot_own, m3t, inv_own, inv_partner, out):
-    leaf, agg = place[0], place[1]
+        target[:, c] = base[:, c] + (dot(high, hot2[:, c]) + dot(low, hot2[:, c]))
+
+
+def group_columns(dim, place):
     span = 2 * dim.elem
-    field = resid[:, pl.ds(pl.multiple_of(leaf * span, span), span)]
+    return pl.ds(pl.multiple_of(place[0] * span, span), span)
+
+
+def group_solve(dim, place, field, hot_own, m3t, inv_own, inv_partner, out, first):
+    agg = place[1]
     sums = restrict(field, hot_own[...], m3t)
-    out[pl.ds(pl.multiple_of(agg * dim.aggs, dim.aggs), dim.aggs), :] = solve_blocks(
+    out[pl.ds(pl.multiple_of(first + agg * dim.aggs, dim.aggs), dim.aggs), :] = solve_blocks(
         sums, 0, inv_own, dim.aggs
     )
-    out[pl.ds(pl.multiple_of((1 - agg) * dim.aggs, dim.aggs), dim.aggs), :] = solve_blocks(
+    out[pl.ds(pl.multiple_of(first + (1 - agg) * dim.aggs, dim.aggs), dim.aggs), :] = solve_blocks(
         sums, dim.aggs, inv_partner, dim.aggs
     )
 
 
-def first_step(dim, source, image, consts, v3, uy, resid, search, scal):
-    def emit(c, value):
-        image[:, c] = value
-
-    apply_operator(dim, search, consts, v3, uy, emit)
-    energy = total(source[...] * search[...])
-    step = energy / total(search[...] * image[...])
-    resid[...] = source[...] - step * image[...]
-    scal[0:1, :] = jnp.broadcast_to(energy, (1, 128))
-    scal[1:2, :] = jnp.broadcast_to(step, (1, 128))
-
-
-def second_step(dim, resid, search, precon, scal, consts, v3, uy, image):
-    energy = total(resid[...] * precon[...])
-    ratio = energy / scal[0:1, 0:1]
-    precon[...] = precon[...] + ratio * search[...]
-
-    def emit(c, value):
-        image[:, c] = value
-
-    apply_operator(dim, precon, consts, v3, uy, emit)
-    step = energy / total(precon[...] * image[...])
-    precon[...] = scal[1:2, 0:1] * search[...] + step * precon[...]
-
-
-def gather_parts(dim, place, parts, solved):
+def inner(dim, left, right):
+    return total(sum(left[:, c] * right[:, c] for c in chunks(dim)))
+
+
+def gather_parts(dim, place, parts, tables):
+    width = dim.group * len(tables)
     groups = []
     for ref in parts:
         first = dim.ndof + 8 if ref.shape[0] > dim.ndof else 0
-        groups += [(ref, step) for step in range(first, ref.shape[0], dim.group)]
+        groups += [(ref, step) for step in range(first, ref.shape[0], width)]
     for index, (ref, first) in enumerate(groups):
         where = place[4 + index] // 2
-        solved[pl.ds(pl.multiple_of(where * dim.group, dim.group), dim.group), :] = ref[
-            first : first + dim.group, :
-        ]
+        rows = pl.ds(pl.multiple_of(where * dim.group, dim.group), dim.group)
+        for number, table in enumerate(tables):
+            start = first + number * dim.group
+            table[rows, :] = ref[start : start + dim.group, :]
 
 
 def begin_kernel(dim, place, source, counts, trsq, lap, g3, gs, gsq3, *refs):
@@ -474,52 +458,97 @@
     apply_operator(dim, start, (visc, fric, lap, g3, gs), v3, uy, emit)
 
 
-def middle_kernel(
-    dim, place, smooth, resid, search, scal, weight, visc, fric, lap, g3, gs, hot2, my, m3t,
-    hot_own, inv_own, inv_partner, *refs,
+def residual_kernel(
+    dim, source, search, image, visc, fric, w_diag, lap, g3, gs, smooth, resid, scal, v3, uy, start
 ):
-    parts = refs[:-8]
-    iterate, source, out, v3, uy, image, solved, precon = refs[-8:]
-    e = dim.elem
-    gather_parts(dim, place, parts, solved)
-    precon[...] = smooth[...]
-    coarse_add(dim, solved[...], my, hot2, precon)
-    consts = (visc, fric, lap, g3, gs)
-    second_step(dim, resid, search, precon, scal, consts, v3, uy, image)
-    mine = pl.ds(pl.multiple_of(place[4] * e, e), e)
-    iterate[...] = precon[:, mine]
-    source[...] = weight[...] * precon[...]
-    group_solve(dim, place, source, hot_own, m3t, inv_own, inv_partner, out)
+    energy = inner(dim, source, search)
+    step = energy / inner(dim, search, image)
+    scal[0:1, :] = jnp.broadcast_to(energy, (1, 128))
+    scal[1:2, :] = jnp.broadcast_to(step, (1, 128))
+    for c in chunks(dim):
+        value = source[:, c] - step * image[:, c]
+        resid[:, c] = value
+        start[:, c] = w_diag[:, c] * value
+
+    def emit(c, image_part):
+        smooth[:, c] = start[:, c] + w_diag[:, c] * (resid[:, c] - image_part)
+
+    apply_operator(dim, start, (visc, fric, lap, g3, gs), v3, uy, emit)
 
 
 def step_kernel(
-    dim, place, smooth, source, visc, fric, lap, g3, gs, hot2, my, m3t, hot_own, inv_own,
+    dim, place, smooth, visc, fric, lap, g3, gs, hot2, my, m3t, hot_own, inv_own,
     inv_partner, *refs,
 ):
-    parts = refs[:-8]
-    search, resid, scal, out, v3, uy, image, solved = refs[-8:]
-    gather_parts(dim, place, parts, solved)
-    search[...] = smooth[...]
-    coarse_add(dim, solved[...], my, hot2, search)
-    consts = (visc, fric, lap, g3, gs)
-    first_step(dim, source, image, consts, v3, uy, resid, search, scal)
-    group_solve(dim, place, resid, hot_own, m3t, inv_own, inv_partner, out)
-
-
-def final_kernel(
-    dim, place, smooth, resid, search, scal, source, sens, visc, fric, lap, g3, gs, hot2, my, *refs
+    parts = refs[:-6]
+    search, image, out, solved, v3, uy = refs[-6:]
+    gather_parts(dim, place, parts, [solved])
+    coarse_add(dim, solved[...], my, hot2, smooth, search)
+
+    def emit(c, value):
+        image[:, c] = value
+
+    apply_operator(dim, search, (visc, fric, lap, g3, gs), v3, uy, emit)
+    field = image[:, group_columns(dim, place)]
+    group_solve(dim, place, field, hot_own, m3t, inv_own, inv_partner, out, 0)
+
+
+def turn(dim, place, parts, smooth, resid, search, scal, solved, my, hot2, table, direction):
+    gather_parts(dim, place, parts, [table])
+    now = solved[...] - scal[1:2, 0:1] * table[...]
+    coarse_add(dim, now, my, hot2, smooth, direction)
+    energy = inner(dim, resid, direction)
+    ratio = energy / scal[0:1, 0:1]
+    for c in chunks(dim):
+        direction[:, c] = direction[:, c] + ratio * search[:, c]
+    return energy
+
+
+def last_step(dim, energy, direction, consts, v3, uy):
+    sums = []
+
+    def emit(c, value):
+        sums.append(jnp.sum(direction[:, c] * value, axis=0, keepdims=True))
+
+    apply_operator(dim, direction, consts, v3, uy, emit)
+    return energy / total(sum(sums))
+
+
+def middle_kernel(
+    dim, place, smooth, resid, search, scal, solved, weight, visc, fric, lap, g3, gs, hot2, my,
+    m3t, hot_own, inv_own, inv_partner, *refs,
 ):
     parts = refs[:-7]
-    action, trace, v3, uy, image, solved, precon = refs[-7:]
-    e = dim.elem
-    gather_parts(dim, place, parts, solved)
-    precon[...] = smooth[...]
-    coarse_add(dim, solved[...], my, hot2, precon)
-    consts = (visc, fric, lap, g3, gs)
-    second_step(dim, resid, search, precon, scal, consts, v3, uy, image)
-    mine = pl.ds(pl.multiple_of(place[4] * e, e), e)
-    action[...] = sens[...] * precon[:, mine]
-    trace[...] = jnp.broadcast_to(total(source[...] * precon[...]), (1, 128))
+    iterate, source, out, v3, uy, table, direction = refs[-7:]
+    energy = turn(
+        dim, place, parts, smooth, resid, search, scal, solved, my, hot2, table, direction
+    )
+    step = last_step(dim, energy, direction, (visc, fric, lap, g3, gs), v3, uy)
+    first = scal[1:2, 0:1]
+    for c in chunks(dim):
+        source[:, c] = weight[:, c] * (first * search[:, c] + step * direction[:, c])
+    mine = pl.ds(pl.multiple_of(place[4] * dim.elem, dim.elem), dim.elem)
+    iterate[...] = first * search[:, mine] + step * direction[:, mine]
+    field = source[:, group_columns(dim, place)]
+    group_solve(dim, place, field, hot_own, m3t, inv_own, inv_partner, out, 0)
+
+
+def final_kernel(
+    dim, place, smooth, resid, search, scal, solved, source, sens, visc, fric, lap, g3, gs, hot2,
+    my, *refs,
+):
+    parts = refs[:-6]
+    action, trace, v3, uy, table, direction = refs[-6:]
+    energy = turn(
+        dim, place, parts, smooth, resid, search, scal, solved, my, hot2, table, direction
+    )
+    with_search = inner(dim, source, search)
+    with_direction = inner(dim, source, direction)
+    step = last_step(dim, energy, direction, (visc, fric, lap, g3, gs), v3, uy)
+    first = scal[1:2, 0:1]
+    mine = pl.ds(pl.multiple_of(place[4] * dim.elem, dim.elem), dim.elem)
+    trace[...] = jnp.broadcast_to(first * with_search + step * with_direction, (1, 128))
+    action[...] = sens[...] * (first * search[:, mine] + step * direction[:, mine])
 
 
 def replicated(
@@ -650,6 +679,8 @@
         flops=2 * once,
     )
 
+    consts = [visc, fric, w_diag, lap, g3, gs]
+
     def sweep_of(first, args):
         (found,) = call(
             lambda *refs: sweep_kernel(dim, first, *refs),
@@ -660,56 +691,68 @@
         )
         return found
 
-    def smooth_and_spread(value, solved_group):
-        consts = [value, visc, fric, w_diag, lap, g3, gs]
-        smooth, found = None, solved_group
-        parts = [solved_group]
-        for sweep in range(SWEEPS - 1):
-            width = 2**sweep
-            if width < leaf_count:
-                pairs = [(index, index ^ width) for index in range(leaf_count)]
-                other = lax.ppermute(found, "leaf", pairs)
-                parts.append(other)
-                if 2 * width < leaf_count:
-                    found = jnp.concatenate([found, other], axis=0)
-            smooth = sweep_of(sweep == 0, consts if sweep == 0 else consts + [smooth])
-        return smooth, parts
-
-    def step_of(smooth, start, parts):
+    def double(parts):
+        width = 2 ** (len(parts) - 1)
+        if width >= leaf_count:
+            return parts
+        pairs = [(index, index ^ width) for index in range(leaf_count)]
+        found = jnp.concatenate(parts, axis=0) if len(parts) > 1 else parts[0]
+        return parts + [lax.ppermute(found, "leaf", pairs)]
+
+    def step_of(smooth, parts):
+        args = [place, smooth, visc, fric, lap, g3, gs, hot2, my, m3t, hot_own, inv_own]
+        args += [inv_partner] + parts
         return call(
             lambda *refs: step_kernel(dim, *refs),
-            [field, field, scal_shape, out_shape],
-            [place, smooth, start, visc, fric, lap, g3, gs, hot2, my, m3t, hot_own, inv_own]
-            + [inv_partner]
-            + parts,
-            [SM] + [VM] * (13 + len(parts)),
-            scratch=work + [image, solved],
+            [field, field, out_shape, table_shape],
+            args,
+            [SM] + [VM] * (len(args) - 1),
+            scratch=work,
             flops=once,
         )
 
-    search, resid, scal, out = step_of(smooth, source, parts)
-    smooth, parts = smooth_and_spread(resid, out)
+    def residual_of(source, search, image_of):
+        return call(
+            lambda *refs: residual_kernel(dim, *refs),
+            [field, field, scal_shape],
+            [source, search, image_of] + consts,
+            scratch=work + [image],
+            flops=once,
+        )
+
+    table_shape = ((dim.all_aggs, dim.modes), f32)
+    search, image_of, out, solved_now = step_of(smooth, parts)
+    parts = double([out])
+    smooth, resid, scal = residual_of(source, search, image_of)
+    parts = double(parts)
+    smooth = sweep_of(False, [resid] + consts + [smooth])
+    args = [place, smooth, resid, search, scal, solved_now, weight, visc, fric, lap, g3, gs]
+    args += [hot2, my, m3t, hot_own, inv_own, inv_partner] + parts
     iterate, source_two, out = call(
         lambda *refs: middle_kernel(dim, *refs),
         [((n, e), f32), field, out_shape],
-        [place, smooth, resid, search, scal, weight, visc, fric, lap, g3, gs, hot2, my]
-        + [m3t, hot_own, inv_own, inv_partner]
-        + parts,
-        [SM] + [VM] * (16 + len(parts)),
-        scratch=work + [image, solved, image],
+        args,
+        [SM] + [VM] * (len(args) - 1),
+        scratch=work + [solved, image],
         flops=once,
     )
-    smooth, parts = smooth_and_spread(source_two, out)
-    search, resid, scal, out = step_of(smooth, source_two, parts)
-    smooth, parts = smooth_and_spread(resid, out)
+    parts = double([out])
+    smooth = sweep_of(True, [source_two] + consts)
+    parts = double(parts)
+    smooth = sweep_of(False, [source_two] + consts + [smooth])
+    search, image_of, out, solved_now = step_of(smooth, parts)
+    parts = double([out])
+    smooth, resid, scal = residual_of(source_two, search, image_of)
+    parts = double(parts)
+    smooth = sweep_of(False, [resid] + consts + [smooth])
+    args = [place, smooth, resid, search, scal, solved_now, source, sensitivity]
+    args += [visc, fric, lap, g3, gs, hot2, my] + parts
     action, trace = call(
         lambda *refs: final_kernel(dim, *refs),
         [((n, e), f32), ((1, 128), f32)],
-        [place, smooth, resid, search, scal, source, sensitivity, visc, fric, lap, g3, gs, hot2]
-        + [my]
-        + parts,
-        [SM] + [VM] * (13 + len(parts)),
-        scratch=work + [image, solved, image],
+        args,
+        [SM] + [VM] * (len(args) - 1),
+        scratch=work + [solved, image],
         flops=once,
     )
     probe_count = lax.axis_size("probe")

time: 98.6 us -> 97.5 us (0.989)
  waiting for transfers between devices: 29.5 us -> 27.4 us
    ppermute x6, waiting for transfers between devices: 5.38 us -> 3.78 us  [double(): return parts + [lax.ppermute(found, 'leaf', pairs)]]
  transfers between devices with their start and end apart: 28 -> 28, of which waited for: 18 -> 18; matrix products, arithmetic and copies ran while one was open for 0% -> 0% of each run, Pallas kernels for 16% -> 17%
where the time goes in v2:
time: 97.5 us; the launch traced here: 97.3 us
  Pallas kernels  41 us (42%)
  waiting for transfers between devices  27.4 us (28%)
  starting transfers between devices  26.8 us (27%)
  between operations  2.05 us (2%)
    pallas_call x15, Pallas kernels, kernel_call(): pl.pallas_call(kernel, out_shape=[jax.ShapeDtypeStruct(*one) for one in o...  41 us
    ppermute x6, starting transfers between devices, peers(): found.append(lax.ppermute(value, 'leaf', pairs))  9.8 us
    ppermute x6, waiting for transfers between devices, peers(): found.append(lax.ppermute(value, 'leaf', pairs))  9.68 us
    ppermute x6, starting transfers between devices, double(): return parts + [lax.ppermute(found, 'leaf', pairs)]  8.16 us
    ppermute x3, waiting for transfers between devices, replicated(): stacks.append(lax.ppermute(stack, 'probe', pairs))  6.49 us
    ppermute x3, waiting for transfers between devices, replicated(): traces.append(lax.ppermute(trace, 'probe', pairs))  3.79 us
    ppermute x6, waiting for transfers between devices, double(): return parts + [lax.ppermute(found, 'leaf', pairs)]  3.78 us
    ppermute x10, waiting for transfers between devices, to_partner(): return lax.ppermute(value, 'agg', flip)  3.68 us
  transfers between devices with their start and end apart: 28, of which 18 were waited for; matrix products, arithmetic and copies ran while one was open for 0% of the time, Pallas kernels for 17%

profile of v2, /device:TPU:0, one launch (start us, length us, event | category | flops | bytes accessed | tf_op | source)
XLA Modules:
  0.0 97.3 jit_solution(2294132088927483189)
XLA Ops:
  0.7 2.7 %shard_map.139 = (f32[200,128]{1,0:T(8,128)S(1)}, f32[144,128]{1,0:T(8,128)S(1)}, f32[128,16]{1,0:T(8,128)S(1)}, bf16[192,576]{1,0:T(8,128)(2,1)S(1)}, bf16[192,...) custom-call(s32[12]{0:T(128)S(1)} %concatenate.12.refs_0_, ...), custom_call_target="tpu_custom_call" | custom-call | flops 100000000 | tf_op jit(solution)/shard_map/pallas_call | solution.py:155
  4.0 4.7 %collective-permute-start.11 = (f32[144,128]{1,0:T(8,128)S(1)}, f32[144,128]{1,0:T(8,128)S(1)}, u32[]{:S(2)}, u32[]{:S(2)}) collective-permute-start(f32[144,128]{1,0:T(8,128)S(1)} %get-tuple-element.52.refs_0_), channel_id=1, source_target_pairs={{0,24},{8,16},{16,8},{24,0},{1,25},{9,17},{17,9},{25,1},{2,26},{10... | collective-permute-start | bytes 221192 | tf_op jit(solution)/shard_map/ppermute | solution.py:598
  9.3 2.6 %collective-permute-done.11.refs_3_ = f32[144,128]{1,0:T(8,128)S(1)} collective-permute-done((f32[144,128]{1,0:T(8,128)S(1)}, f32[144,128]{1,0:T(8,128)S(1)}, u32[]{:S(2)}, u32[]{:S(2)}) %collective-permute-start.11) | collective-permute-done | bytes 73760 | tf_op jit(solution)/shard_map/ppermute | solution.py:598
  11.9 3.5 %collective-permute-done.10.refs_2_ = f32[144,128]{1,0:T(8,128)S(1)} collective-permute-done((f32[144,128]{1,0:T(8,128)S(1)}, f32[144,128]{1,0:T(8,128)S(1)}, u32[]{:S(2)}, u32[]{:S(2)}) %collective-permute-start.10) | collective-permute-done | bytes 73760 | tf_op jit(solution)/shard_map/ppermute | solution.py:598
  15.4 2.5 %collective-permute-start.14 = (f32[576,128]{1,0:T(8,128)S(1)}, f32[576,128]{1,0:T(8,128)S(1)}, u32[]{:S(2)}, u32[]{:S(2)}) collective-permute-start(f32[576,128]{1,0:T(8,128)S(1)} %shard_map.142.refs_8_), channel_id=1, source_target_pairs={{0,3},{1,2},{2,1},{3,0},{4,7},{5,6},{6,5},{7,4},{8,11},{9,10},{10,... | collective-permute-start | bytes 884744 | tf_op jit(solution)/shard_map/ppermute | solution.py:639
  21.3 2.5 %collective-permute-start.4 = (f32[216,128]{1,0:T(8,128)S(1)}, f32[216,128]{1,0:T(8,128)S(1)}, u32[]{:S(2)}, u32[]{:S(2)}) collective-permute-start(f32[216,128]{1,0:T(8,128)S(1)} %shard_map.140.refs_1_.refs_13_), channel_id=1, source_target_pairs={{0,24},{8,16},{16,8},{24,0},{1,25},{9,17},{17,9},{25,1},{2,26},{10... | collective-permute-start | bytes 331784 | tf_op jit(solution)/shard_map/ppermute | solution.py:598
  23.8 2.5 %collective-permute-done.14.refs_11_ = f32[576,128]{1,0:T(8,128)S(1)} collective-permute-done((f32[576,128]{1,0:T(8,128)S(1)}, f32[576,128]{1,0:T(8,128)S(1)}, u32[]{:S(2)}, u32[]{:S(2)}) %collective-permute-start.14) | collective-permute-done | bytes 294944 | tf_op jit(solution)/shard_map/ppermute | solution.py:639
  27.2 4.0 %collective-permute-done.13.refs_10_ = f32[576,128]{1,0:T(8,128)S(1)} collective-permute-done((f32[576,128]{1,0:T(8,128)S(1)}, f32[576,128]{1,0:T(8,128)S(1)}, u32[]{:S(2)}, u32[]{:S(2)}) %collective-permute-start.13) | collective-permute-done | bytes 294944 | tf_op jit(solution)/shard_map/ppermute | solution.py:639
  34.1 2.3 %collective-permute-done.2.refs_2_.refs_14_ = f32[216,128]{1,0:T(8,128)S(1)} collective-permute-done((f32[216,128]{1,0:T(8,128)S(1)}, f32[216,128]{1,0:T(8,128)S(1)}, u32[]{:S(2)}, u32[]{:S(2)}) %collective-permute-start.2) | collective-permute-done | bytes 110624 | tf_op jit(solution)/shard_map/ppermute | solution.py:598
  39.5 2.3 %shard_map.141 = (f32[192,1024]{1,0:T(8,128)S(1)}, bf16[1024,1024]{1,0:T(8,128)(2,1)S(1)}, bf16[64,1024]{1,0:T(8,128)(2,1)S(1)}, f32[1,1024]{1,0:T(1,128)S(1)}, bf16[16,256]{1,0:T(8,128)(2,1)S(1)}) custom-call(s32[12]{0:T(128)S(1)} %concatenate.12.refs_0_, f32[216,128]{1,0:T(8,128)S(1)} %shard_map.140.refs_1_.refs_13_, ...), custom_call_target="tpu_custom_call" | custom-call | tf_op jit(solution)/shard_map/pallas_call | solution.py:155
  41.9 5.5 %shard_map.143 = (f32[192,1024]{1,0:T(8,128)S(1)}, f32[192,1024]{1,0:T(8,128)S(1)}, f32[192,1024]{1,0:T(8,128)S(1)}, f32[192,1024]{1,0:T(8,128)S(1)}, f32[192,1024]{1,0:T(8,128)S(1)}) custom-call(s32[12]{0:T(128)S(1)} %concatenate.12.refs_0_, f32[192,1024]{1,0:T(8,128)S(1)} %get-tuple-element.45.refs_1_.refs_0_.refs_6_, ...), custom_call_target="tpu_custom_call" | custom-call | flops 2969567232 | tf_op jit(solution)/shard_map/pallas_call | solution.py:155
  47.4 3.7 %shard_map.144 = (f32[192,1024]{1,0:T(8,128)S(1)}, f32[192,1024]{1,0:T(8,128)S(1)}, f32[16,128]{1,0:T(8,128)S(1)}, f32[64,128]{1,0:T(8,128)S(1)}) custom-call(s32[12]{0:T(128)S(1)} %concatenate.12.refs_0_, f32[192,1024]{1,0:T(8,128)S(1)} %get-tuple-element.53.refs_1_, f32[192,1024]{1,0:T(8,128)S(1)} %get-tuple-element.54.refs_2_.refs_3_.refs_1_.refs_7_.refs_8_, ...), custom_call_target="tpu_custom_call" | custom-call | flops 1484783616 | tf_op jit(solution)/shard_map/pallas_call | solution.py:155
  52.0 2.5 %shard_map.145 = (f32[192,1024]{1,0:T(8,128)S(1)}, f32[192,1024]{1,0:T(8,128)S(1)}, f32[8,128]{1,0:T(8,128)S(1)}) custom-call(f32[192,1024]{1,0:T(8,128)S(1)} %get-tuple-element.45.refs_1_.refs_0_.refs_6_, f32[192,1024]{1,0:T(8,128)S(1)} %get-tuple-element.60.refs_1_.refs_3_, f32[192,1024]{1,0:T(8,128)S(1)} %get-tuple-element.61.refs_2_, ...), custom_call_target="tpu_custom_call" | custom-call | flops 1484783616 | tf_op jit(solution)/shard_map/pallas_call | solution.py:155
  54.8 1.8 %collective-permute-start.20 = (f32[32,128]{1,0:T(8,128)S(1)}, f32[32,128]{1,0:T(8,128)S(1)}, u32[]{:S(2)}, u32[]{:S(2)}) collective-permute-start(f32[32,128]{1,0:T(8,128)S(1)} %pad_maximum_fusion), channel_id=1, source_target_pairs={{0,16},{8,24},{16,0},{24,8},{1,17},{9,25},{17,1},{25,9},{2,18},{10... | collective-permute-start | bytes 49160 | tf_op jit(solution)/shard_map/ppermute | solution.py:700
  56.6 2.0 %shard_map.146.refs_1_ = f32[192,1024]{1,0:T(8,128)S(1)} custom-call(f32[192,1024]{1,0:T(8,128)S(1)} %get-tuple-element.63.refs_0_.refs_2_, f32[192,1024]{1,0:T(8,128)S(1)} %get-tuple-element.54.refs_2_.refs_3_.refs_1_.refs_7_.refs_8_, f32[192,1024]{1,0:T(8,128)S(1)} %get-tuple-element.55.refs_3_.refs_4_.refs_2_.refs_8_.refs_9_, ...), custom_call_target="tpu_custom_call" | custom-call | flops 1484783616 | tf_op jit(solution)/shard_map/pallas_call | solution.py:155
  59.4 4.5 %shard_map.147 = (f32[192,128]{1,0:T(8,128)}, f32[192,1024]{1,0:T(8,128)S(1)}, f32[16,128]{1,0:T(8,128)S(1)}) custom-call(s32[12]{0:T(128)S(1)} %concatenate.12.refs_0_, f32[192,1024]{1,0:T(8,128)S(1)} %shard_map.146.refs_1_, f32[192,1024]{1,0:T(8,128)S(1)} %get-tuple-element.63.refs_0_.refs_2_, f32[192,1024]{1,0:T(8,128)S(1)} %get-tuple-element.60.refs_1_.refs_3_, ...), custom_call_target="tpu_custom_call" | custom-call | flops 1484783616 | tf_op jit(solution)/shard_map/pallas_call | solution.py:155
  64.9 2.1 %shard_map.148.refs_7_ = f32[192,1024]{1,0:T(8,128)S(1)} custom-call(f32[192,1024]{1,0:T(8,128)S(1)} %get-tuple-element.70.refs_0_, f32[192,1024]{1,0:T(8,128)S(1)} %get-tuple-element.54.refs_2_.refs_3_.refs_1_.refs_7_.refs_8_, f32[192,1024]{1,0:T(8,128)S(1)} %get-tuple-element.55.refs_3_.refs_4_.refs_2_.refs_8_.refs_9_, ...), custom_call_target="tpu_custom_call" | custom-call | flops 1484783616 | tf_op jit(solution)/shard_map/pallas_call | solution.py:155
  67.6 1.8 %collective-permute-start.22 = (f32[32,128]{1,0:T(8,128)S(1)}, f32[32,128]{1,0:T(8,128)S(1)}, u32[]{:S(2)}, u32[]{:S(2)}) collective-permute-start(f32[32,128]{1,0:T(8,128)S(1)} %pad_maximum_fusion.1), channel_id=1, source_target_pairs={{0,16},{8,24},{16,0},{24,8},{1,17},{9,25},{17,1},{25,9},{2,18},{10... | collective-permute-start | bytes 49160 | tf_op jit(solution)/shard_map/ppermute | solution.py:700
  69.4 2.0 %shard_map.149.refs_1_ = f32[192,1024]{1,0:T(8,128)S(1)} custom-call(f32[192,1024]{1,0:T(8,128)S(1)} %get-tuple-element.70.refs_0_, f32[192,1024]{1,0:T(8,128)S(1)} %get-tuple-element.54.refs_2_.refs_3_.refs_1_.refs_7_.refs_8_, f32[192,1024]{1,0:T(8,128)S(1)} %get-tuple-element.55.refs_3_.refs_4_.refs_2_.refs_8_.refs_9_, ...), custom_call_target="tpu_custom_call" | custom-call | flops 1484783616 | tf_op jit(solution)/shard_map/pallas_call | solution.py:155
  72.3 3.9 %shard_map.150 = (f32[192,1024]{1,0:T(8,128)S(1)}, f32[192,1024]{1,0:T(8,128)S(1)}, f32[16,128]{1,0:T(8,128)S(1)}, f32[64,128]{1,0:T(8,128)S(1)}) custom-call(s32[12]{0:T(128)S(1)} %concatenate.12.refs_0_, f32[192,1024]{1,0:T(8,128)S(1)} %shard_map.149.refs_1_, f32[192,1024]{1,0:T(8,128)S(1)} %get-tuple-element.54.refs_2_.refs_3_.refs_1_.refs_7_.refs_8_, ...), custom_call_target="tpu_custom_call" | custom-call | flops 1484783616 | tf_op jit(solution)/shard_map/pallas_call | solution.py:155
  77.2 2.5 %shard_map.151 = (f32[192,1024]{1,0:T(8,128)S(1)}, f32[192,1024]{1,0:T(8,128)S(1)}, f32[8,128]{1,0:T(8,128)S(1)}) custom-call(f32[192,1024]{1,0:T(8,128)S(1)} %get-tuple-element.70.refs_0_, f32[192,1024]{1,0:T(8,128)S(1)} %get-tuple-element.72.refs_1_.refs_3_, f32[192,1024]{1,0:T(8,128)S(1)} %get-tuple-element.73.refs_2_, ...), custom_call_target="tpu_custom_call" | custom-call | flops 1484783616 | tf_op jit(solution)/shard_map/pallas_call | solution.py:155
  81.7 2.0 %shard_map.152.refs_1_ = f32[192,1024]{1,0:T(8,128)S(1)} custom-call(f32[192,1024]{1,0:T(8,128)S(1)} %get-tuple-element.74.refs_0_.refs_2_, f32[192,1024]{1,0:T(8,128)S(1)} %get-tuple-element.54.refs_2_.refs_3_.refs_1_.refs_7_.refs_8_, f32[192,1024]{1,0:T(8,128)S(1)} %get-tuple-element.55.refs_3_.refs_4_.refs_2_.refs_8_.refs_9_, ...), custom_call_target="tpu_custom_call" | custom-call | flops 1484783616 | tf_op jit(solution)/shard_map/pallas_call | solution.py:155
  84.5 4.2 %shard_map.153 = (f32[192,128]{1,0:T(8,128)}, f32[1,128]{1,0:T(1,128)S(1)}) custom-call(s32[12]{0:T(128)S(1)} %concatenate.12.refs_0_, f32[192,1024]{1,0:T(8,128)S(1)} %shard_map.152.refs_1_, f32[192,1024]{1,0:T(8,128)S(1)} %get-tuple-element.74.refs_0_.refs_2_, f32[192,1024]{1,0:T(8,128)S(1)} %get-tuple-element.72.refs_1_.refs_3_, ...), custom_call_target="tpu_custom_call" | custom-call | flops 1484783616 | tf_op jit(solution)/shard_map/pallas_call | solution.py:155
  93.9 2.3 %collective-permute-done.27 = f32[1,128]{1,0:T(1,128)S(1)} collective-permute-done((f32[1,128]{1,0:T(1,128)S(1)}, f32[1,128]{1,0:T(1,128)S(1)}, u32[]{:S(2)}, u32[]{:S(2)}) %collective-permute-start.27) | collective-permute-done | bytes 544 | tf_op jit(solution)/shard_map/ppermute | solution.py:764
  (54 shorter events, 24.9 us)
Async XLA Ops:
  3.4 16.8 %collective-permute-start.1 = (f32[8,128,128]{2,1,0:T(8,128)S(1)}, f32[8,128,128]{2,1,0:T(8,128)S(1)}, u32[]{:S(2)}, u32[]{:S(2)}) collective-permute-start(f32[8,128,128]{2,1,0:T(8,128)S(1)} %get-tuple-element.44.refs_4_.refs_11_.refs_16_), channel_id=1, source_target_pairs={{0,4},{4,0},{1,5},{5,1},{2,6},{6,2},{3,7},{7,3},{8,12},{12,8},{9,1... | collective-permute-start | bytes 1572872 | tf_op jit(solution)/shard_map/ppermute | solution.py:592
  4.0 7.9 %collective-permute-start.11 = (f32[144,128]{1,0:T(8,128)S(1)}, f32[144,128]{1,0:T(8,128)S(1)}, u32[]{:S(2)}, u32[]{:S(2)}) collective-permute-start(f32[144,128]{1,0:T(8,128)S(1)} %get-tuple-element.52.refs_0_), channel_id=1, source_target_pairs={{0,24},{8,16},{16,8},{24,0},{1,25},{9,17},{17,9},{25,1},{2,26},{10... | collective-permute-start | bytes 221192 | tf_op jit(solution)/shard_map/ppermute | solution.py:598
  8.7 6.8 %collective-permute-start.10 = (f32[144,128]{1,0:T(8,128)S(1)}, f32[144,128]{1,0:T(8,128)S(1)}, u32[]{:S(2)}, u32[]{:S(2)}) collective-permute-start(f32[144,128]{1,0:T(8,128)S(1)} %get-tuple-element.52.refs_0_), channel_id=1, source_target_pairs={{0,16},{8,24},{16,0},{24,8},{1,17},{9,25},{17,1},{25,9},{2,18},{10... | collective-permute-start | bytes 221192 | tf_op jit(solution)/shard_map/ppermute | solution.py:598
  8.7 6.8 %collective-permute-start.9 = (f32[144,128]{1,0:T(8,128)S(1)}, f32[144,128]{1,0:T(8,128)S(1)}, u32[]{:S(2)}, u32[]{:S(2)}) collective-permute-start(f32[144,128]{1,0:T(8,128)S(1)} %get-tuple-element.52.refs_0_), channel_id=1, source_target_pairs={{0,8},{8,0},{16,24},{24,16},{1,9},{9,1},{17,25},{25,17},{2,10},{10... | collective-permute-start | bytes 221192 | tf_op jit(solution)/shard_map/ppermute | solution.py:598
  15.4 10.9 %collective-permute-start.14 = (f32[576,128]{1,0:T(8,128)S(1)}, f32[576,128]{1,0:T(8,128)S(1)}, u32[]{:S(2)}, u32[]{:S(2)}) collective-permute-start(f32[576,128]{1,0:T(8,128)S(1)} %shard_map.142.refs_8_), channel_id=1, source_target_pairs={{0,3},{1,2},{2,1},{3,0},{4,7},{5,6},{6,5},{7,4},{8,11},{9,10},{10,... | collective-permute-start | bytes 884744 | tf_op jit(solution)/shard_map/ppermute | solution.py:639
  18.0 13.3 %collective-permute-start.13 = (f32[576,128]{1,0:T(8,128)S(1)}, f32[576,128]{1,0:T(8,128)S(1)}, u32[]{:S(2)}, u32[]{:S(2)}) collective-permute-start(f32[576,128]{1,0:T(8,128)S(1)} %shard_map.142.refs_8_), channel_id=1, source_target_pairs={{0,2},{1,3},{2,0},{3,1},{4,6},{5,7},{6,4},{7,5},{8,10},{9,11},{10,... | collective-permute-start | bytes 884744 | tf_op jit(solution)/shard_map/ppermute | solution.py:639
  18.5 13.8 %collective-permute-start.12 = (f32[576,128]{1,0:T(8,128)S(1)}, f32[576,128]{1,0:T(8,128)S(1)}, u32[]{:S(2)}, u32[]{:S(2)}) collective-permute-start(f32[576,128]{1,0:T(8,128)S(1)} %shard_map.142.refs_8_), channel_id=1, source_target_pairs={{0,1},{1,0},{2,3},{3,2},{4,5},{5,4},{6,7},{7,6},{8,9},{9,8},{10,11... | collective-permute-start | bytes 884744 | tf_op jit(solution)/shard_map/ppermute | solution.py:639
  21.3 11.0 %collective-permute-start.4 = (f32[216,128]{1,0:T(8,128)S(1)}, f32[216,128]{1,0:T(8,128)S(1)}, u32[]{:S(2)}, u32[]{:S(2)}) collective-permute-start(f32[216,128]{1,0:T(8,128)S(1)} %shard_map.140.refs_1_.refs_13_), channel_id=1, source_target_pairs={{0,24},{8,16},{16,8},{24,0},{1,25},{9,17},{17,9},{25,1},{2,26},{10... | collective-permute-start | bytes 331784 | tf_op jit(solution)/shard_map/ppermute | solution.py:598
  23.8 9.0 %collective-permute-start.5 = (f32[216,128]{1,0:T(8,128)S(1)}, f32[216,128]{1,0:T(8,128)S(1)}, u32[]{:S(2)}, u32[]{:S(2)}) collective-permute-start(f32[216,128]{1,0:T(8,128)S(1)} %shard_map.140.refs_1_.refs_13_), channel_id=1, source_target_pairs={{0,4},{4,0},{1,5},{5,1},{2,6},{6,2},{3,7},{7,3},{8,12},{12,8},{9,1... | collective-permute-start | bytes 331784 | tf_op jit(solution)/shard_map/ppermute | solution.py:592
  26.3 7.7 %collective-permute-start.3 = (f32[216,128]{1,0:T(8,128)S(1)}, f32[216,128]{1,0:T(8,128)S(1)}, u32[]{:S(2)}, u32[]{:S(2)}) collective-permute-start(f32[216,128]{1,0:T(8,128)S(1)} %shard_map.140.refs_1_.refs_13_), channel_id=1, source_target_pairs={{0,16},{8,24},{16,0},{24,8},{1,17},{9,25},{17,1},{25,9},{2,18},{10... | collective-permute-start | bytes 331784 | tf_op jit(solution)/shard_map/ppermute | solution.py:598
  31.2 5.2 %collective-permute-start.2 = (f32[216,128]{1,0:T(8,128)S(1)}, f32[216,128]{1,0:T(8,128)S(1)}, u32[]{:S(2)}, u32[]{:S(2)}) collective-permute-start(f32[216,128]{1,0:T(8,128)S(1)} %shard_map.140.refs_1_.refs_13_), channel_id=1, source_target_pairs={{0,8},{8,0},{16,24},{24,16},{1,9},{9,1},{17,25},{25,17},{2,10},{10... | collective-permute-start | bytes 331784 | tf_op jit(solution)/shard_map/ppermute | solution.py:598
  32.3 4.2 %collective-permute-start.8 = (f32[216,128]{1,0:T(8,128)S(1)}, f32[216,128]{1,0:T(8,128)S(1)}, u32[]{:S(2)}, u32[]{:S(2)}) collective-permute-start(f32[216,128]{1,0:T(8,128)S(1)} %collective-permute-done.4.refs_4_.refs_16_), channel_id=1, source_target_pairs={{0,4},{4,0},{1,5},{5,1},{2,6},{6,2},{3,7},{7,3},{8,12},{12,8},{9,1... | collective-permute-start | bytes 331784 | tf_op jit(solution)/shard_map/ppermute | solution.py:592
  32.3 9.6 %collective-permute-start.15 = (f32[576,128]{1,0:T(8,128)S(1)}, f32[576,128]{1,0:T(8,128)S(1)}, u32[]{:S(2)}, u32[]{:S(2)}) collective-permute-start(f32[576,128]{1,0:T(8,128)S(1)} %shard_map.142.refs_8_), channel_id=1, source_target_pairs={{0,4},{4,0},{1,5},{5,1},{2,6},{6,2},{3,7},{7,3},{8,12},{12,8},{9,1... | collective-permute-start | bytes 884744 | tf_op jit(solution)/shard_map/ppermute | solution.py:592
  32.8 9.1 %collective-permute-start.18 = (f32[576,128]{1,0:T(8,128)S(1)}, f32[576,128]{1,0:T(8,128)S(1)}, u32[]{:S(2)}, u32[]{:S(2)}) collective-permute-start(f32[576,128]{1,0:T(8,128)S(1)} %collective-permute-done.14.refs_11_), channel_id=1, source_target_pairs={{0,4},{4,0},{1,5},{5,1},{2,6},{6,2},{3,7},{7,3},{8,12},{12,8},{9,1... | collective-permute-start | bytes 884744 | tf_op jit(solution)/shard_map/ppermute | solution.py:592
  34.1 7.8 %collective-permute-start.17 = (f32[576,128]{1,0:T(8,128)S(1)}, f32[576,128]{1,0:T(8,128)S(1)}, u32[]{:S(2)}, u32[]{:S(2)}) collective-permute-start(f32[576,128]{1,0:T(8,128)S(1)} %collective-permute-done.13.refs_10_), channel_id=1, source_target_pairs={{0,4},{4,0},{1,5},{5,1},{2,6},{6,2},{3,7},{7,3},{8,12},{12,8},{9,1... | collective-permute-start | bytes 884744 | tf_op jit(solution)/shard_map/ppermute | solution.py:592
  36.4 5.4 %collective-permute-start.16 = (f32[576,128]{1,0:T(8,128)S(1)}, f32[576,128]{1,0:T(8,128)S(1)}, u32[]{:S(2)}, u32[]{:S(2)}) collective-permute-start(f32[576,128]{1,0:T(8,128)S(1)} %collective-permute-done.12.refs_9_), channel_id=1, source_target_pairs={{0,4},{4,0},{1,5},{5,1},{2,6},{6,2},{3,7},{7,3},{8,12},{12,8},{9,1... | collective-permute-start | bytes 884744 | tf_op jit(solution)/shard_map/ppermute | solution.py:592
  51.1 3.7 %collective-permute-start.19 = (f32[16,128]{1,0:T(8,128)S(1)}, f32[16,128]{1,0:T(8,128)S(1)}, u32[]{:S(2)}, u32[]{:S(2)}) collective-permute-start(f32[16,128]{1,0:T(8,128)S(1)} %get-tuple-element.68.refs_18_), channel_id=1, source_target_pairs={{0,8},{8,0},{16,24},{24,16},{1,9},{9,1},{17,25},{25,17},{2,10},{10... | collective-permute-start | bytes 24584 | tf_op jit(solution)/shard_map/ppermute | solution.py:700
  54.8 4.6 %collective-permute-start.20 = (f32[32,128]{1,0:T(8,128)S(1)}, f32[32,128]{1,0:T(8,128)S(1)}, u32[]{:S(2)}, u32[]{:S(2)}) collective-permute-start(f32[32,128]{1,0:T(8,128)S(1)} %pad_maximum_fusion), channel_id=1, source_target_pairs={{0,16},{8,24},{16,0},{24,8},{1,17},{9,25},{17,1},{25,9},{2,18},{10... | collective-permute-start | bytes 49160 | tf_op jit(solution)/shard_map/ppermute | solution.py:700
  63.9 3.7 %collective-permute-start.21 = (f32[16,128]{1,0:T(8,128)S(1)}, f32[16,128]{1,0:T(8,128)S(1)}, u32[]{:S(2)}, u32[]{:S(2)}) collective-permute-start(f32[16,128]{1,0:T(8,128)S(1)} %get-tuple-element.71.refs_13_), channel_id=1, source_target_pairs={{0,8},{8,0},{16,24},{24,16},{1,9},{9,1},{17,25},{25,17},{2,10},{10... | collective-permute-start | bytes 24584 | tf_op jit(solution)/shard_map/ppermute | solution.py:700
  67.6 4.6 %collective-permute-start.22 = (f32[32,128]{1,0:T(8,128)S(1)}, f32[32,128]{1,0:T(8,128)S(1)}, u32[]{:S(2)}, u32[]{:S(2)}) collective-permute-start(f32[32,128]{1,0:T(8,128)S(1)} %pad_maximum_fusion.1), channel_id=1, source_target_pairs={{0,16},{8,24},{16,0},{24,8},{1,17},{9,25},{17,1},{25,9},{2,18},{10... | collective-permute-start | bytes 49160 | tf_op jit(solution)/shard_map/ppermute | solution.py:700
  76.2 3.7 %collective-permute-start.23 = (f32[16,128]{1,0:T(8,128)S(1)}, f32[16,128]{1,0:T(8,128)S(1)}, u32[]{:S(2)}, u32[]{:S(2)}) collective-permute-start(f32[16,128]{1,0:T(8,128)S(1)} %get-tuple-element.78.refs_15_), channel_id=1, source_target_pairs={{0,8},{8,0},{16,24},{24,16},{1,9},{9,1},{17,25},{25,17},{2,10},{10... | collective-permute-start | bytes 24584 | tf_op jit(solution)/shard_map/ppermute | solution.py:700
  79.9 4.6 %collective-permute-start.24 = (f32[32,128]{1,0:T(8,128)S(1)}, f32[32,128]{1,0:T(8,128)S(1)}, u32[]{:S(2)}, u32[]{:S(2)}) collective-permute-start(f32[32,128]{1,0:T(8,128)S(1)} %pad_maximum_fusion.2), channel_id=1, source_target_pairs={{0,16},{8,24},{16,0},{24,8},{1,17},{9,25},{17,1},{25,9},{2,18},{10... | collective-permute-start | bytes 49160 | tf_op jit(solution)/shard_map/ppermute | solution.py:700
  88.8 3.6 %collective-permute-start.25 = (f32[1,128]{1,0:T(1,128)S(1)}, f32[1,128]{1,0:T(1,128)S(1)}, u32[]{:S(2)}, u32[]{:S(2)}) collective-permute-start(f32[1,128]{1,0:T(1,128)S(1)} %get-tuple-element.80), channel_id=1, source_target_pairs={{0,1},{1,0},{2,3},{3,2},{4,5},{5,4},{6,7},{7,6},{8,9},{9,8},{10,11... | collective-permute-start | bytes 1544 | tf_op jit(solution)/shard_map/ppermute | solution.py:764
  91.7 4.5 %collective-permute-start.27 = (f32[1,128]{1,0:T(1,128)S(1)}, f32[1,128]{1,0:T(1,128)S(1)}, u32[]{:S(2)}, u32[]{:S(2)}) collective-permute-start(f32[1,128]{1,0:T(1,128)S(1)} %get-tuple-element.80), channel_id=1, source_target_pairs={{0,3},{1,2},{2,1},{3,0},{4,7},{5,6},{6,5},{7,4},{8,11},{9,10},{10,... | collective-permute-start | bytes 1544 | tf_op jit(solution)/shard_map/ppermute | solution.py:764
  (5 other events, 10.8 us)
